TPU v7x, 32 devices: a whole 2x2x4 slice. The times are simulated.
32 devices in a mesh: dp: 8 (over z, x), pipe: 4 (over y, core).
Axes of the slice: x: 2, y: 2, z: 4, core: 2. Of those that a mesh axis runs over, the one named last changes fastest.
Arguments:
- noise_draw: bfloat16 [2, 14976, 128], P(None, 'dp'), may hold values from -6 to 6
- single_step: bfloat16 [2, 14976, 128], P(None, 'dp'), may hold values from -6 to 6
- double_step: bfloat16 [2, 14976, 128], P(None, 'dp'), may hold values from -6 to 6
- state_now: bfloat16 [2, 14976, 128], P(None, 'dp'), may hold values from -6 to 6
- target_flag: int32 [2, 8], P(None, 'dp'), may hold values from 0 to 1
- flow_time: float32 [2, 8], P(None, 'dp'), may hold values from 0.05 to 0.95
- live_count: int32 [2, 8], P(None, 'dp'), may hold values from 507 to 1872, as said below
- latitude_row: int32 [2, 1152], P(None, 'dp'), may hold values from 0 to 59
- window_order: int32 [2, 14976], P(None, 'dp'), may hold values from 0 to 1871, as said below
- latitude_weight: int32 [60], replicated, may hold values from 100 to 1000
- level_weight: int32 [13], replicated, may hold values from 100 to 1000
- step_count: int32 [1], replicated, may hold values from 2 to 20
- master_weights: float32 [6528, 384], P('dp')
- first_moment: float32 [6528, 384], P('dp')
- second_moment: float32 [6528, 384], P('dp')
- average_weights: float32 [6528, 384], P('dp')
- gain_rows: float32 [5, 384], replicated
- gain_first: float32 [5, 384], replicated
- gain_second: float32 [5, 384], replicated
- gain_average: float32 [5, 384], replicated
Outputs:
- loss_value: float32 [], replicated
- grad_norm: float32 [], replicated
- new_weights: float32 [6528, 384], P('dp')
- new_first: float32 [6528, 384], P('dp')
- new_second: float32 [6528, 384], P('dp')
- new_average: float32 [6528, 384], P('dp')
- weights_low: bfloat16 [6528, 384], P('dp')
- new_gains: float32 [5, 384], replicated
- new_gain_first: float32 [5, 384], replicated
- new_gain_second: float32 [5, 384], replicated
- new_gain_average: float32 [5, 384], replicated
Inputs may be any that keep to these rules, and one draw needn't show every extreme that they name: `window_order`: each index of dp and micro-batch holds its own block of 1872 entries, a permutation of 0 to 1871 naming the block's own patches. `live_count`: the first that many patches of a block count; it rises along dp, and the last index of dp holds 1872 in every micro-batch.
All inputs are finite; a program needn't handle non-finite values.
Results may differ from a plain program's by a relative error of at most 0.0038.
Values may be sent and summed in bfloat16 or wider, within the bound.
A program may use at most 256 MiB of HBM per device.

v0:
```python
import jax
import jax.numpy as jnp
from jax import lax
from jax.sharding import PartitionSpec as P

D = 384
HEADS = 12
HD = 32
FF = 1536
PIN = 128
LEV = 13
WSZ = 144
LATN = 60


EPS_NORM = 1e-05
CLIP_MAX = 0.01
RATE = 0.03
GAIN_RATE = 0.3
BETA = 0.5
EPS_ADAM = 1e-08
DECAY_WEIGHT = 0.05
EMA_RATE = 0.8


def as_sent(value):

    def short(part):
        return part.astype(jnp.bfloat16) if part.dtype == jnp.float32 else part

    return jax.tree.map(short, value)


def passed_along(value, axis, by):
    length = lax.axis_size(axis)
    pairs = [(i, i + by) for i in range(length) if 0 <= i + by < length]
    return lax.ppermute(value, axis, pairs)


def block_starts():
    widths = [2 * PIN, 3 * D, D, FF, FF, 3 * D, D, PIN]
    starts = [0]
    for width in widths:
        starts.append(starts[-1] + width)
    return starts


def natural_order(stored, pieces_count):
    starts = block_starts()
    view = stored.reshape(pieces_count, stored.shape[0] // pieces_count, stored.shape[1])
    pieces = []
    for number in range(8):
        pieces.append(
            view[:, starts[number] // pieces_count : starts[number + 1] // pieces_count].reshape(
                -1, stored.shape[1]
            )
        )
    return jnp.concatenate(pieces, axis=0)


def stored_order(natural, pieces_count):
    starts = block_starts()
    pieces = []
    for number in range(8):
        pieces.append(
            natural[starts[number] : starts[number + 1]].reshape(pieces_count, -1, natural.shape[1])
        )
    return jnp.concatenate(pieces, axis=1).reshape(-1, natural.shape[1])


def matmul(left, right):
    return jnp.dot(left, right, preferred_element_type=jnp.float32)


def matmul_nt(left, right):
    return lax.dot_general(
        left, right, (((1,), (1,)), ((), ())), preferred_element_type=jnp.float32
    )


def matmul_tn(left, right):
    return lax.dot_general(
        left, right, (((0,), (0,)), ((), ())), preferred_element_type=jnp.float32
    )


def layer_norm(values, scaling):
    center = values - jnp.mean(values, axis=-1, keepdims=True)
    return (
        center * lax.rsqrt(jnp.mean(center * center, axis=-1, keepdims=True) + EPS_NORM) * scaling
    )


def norm_back(values, scaling, upstream):
    _, pullback = jax.vjp(layer_norm, values, scaling)
    return pullback(upstream)


def attend_weights(query, keys):
    scores = jnp.einsum(
        "gqhe,gkhe->ghqk", query, keys, preferred_element_type=jnp.float32
    ) * HD ** (-0.5)
    top = jnp.max(scores, axis=-1, keepdims=True)
    expo = jnp.exp(scores - top)
    return expo / jnp.sum(expo, axis=-1, keepdims=True)


def attend_forward(query, keys, values):
    weights_p = attend_weights(query, keys).astype(jnp.bfloat16)
    return jnp.einsum(
        "ghqk,gkhe->gqhe", weights_p, values, preferred_element_type=jnp.float32
    ).astype(jnp.bfloat16)


def attend_backward(query, keys, values, grad_context):
    weights_p = attend_weights(query, keys)
    grad_values = jnp.einsum(
        "ghqk,gqhe->gkhe",
        weights_p.astype(jnp.bfloat16),
        grad_context,
        preferred_element_type=jnp.float32,
    )
    grad_weights = jnp.einsum(
        "gqhe,gkhe->ghqk", grad_context, values, preferred_element_type=jnp.float32
    )
    grad_scores = (
        weights_p * (grad_weights - jnp.sum(grad_weights * weights_p, axis=-1, keepdims=True))
    ).astype(jnp.bfloat16)
    factor = HD ** (-0.5)
    grad_query = (
        jnp.einsum("ghqk,gkhe->gqhe", grad_scores, keys, preferred_element_type=jnp.float32)
        * factor
    )
    grad_keys = (
        jnp.einsum("ghqk,gqhe->gkhe", grad_scores, query, preferred_element_type=jnp.float32)
        * factor
    )
    return jnp.stack([grad_query, grad_keys, grad_values], axis=2)


def swin_forward(hidden_in, order, weights, gain_rows):
    starts = block_starts()
    hidden = hidden_in.astype(jnp.float32)
    normed = layer_norm(hidden, gain_rows[0]).astype(jnp.bfloat16)
    triple = matmul_nt(normed, weights[starts[1] : starts[2]]).astype(jnp.bfloat16)
    windows = triple[order].reshape(-1, WSZ, 3, HEADS, HD)
    context = attend_forward(windows[:, :, 0], windows[:, :, 1], windows[:, :, 2]).reshape(-1, D)
    inverse = jnp.zeros_like(order).at[order].set(jnp.arange(order.shape[0], dtype=jnp.int32))
    mixed = hidden + matmul(context, weights[starts[2] : starts[3]])[inverse]
    second = layer_norm(mixed, gain_rows[1]).astype(jnp.bfloat16)
    upper = matmul_nt(second, weights[starts[3] : starts[4]])
    active = jax.nn.gelu(upper).astype(jnp.bfloat16)
    result = (mixed + matmul(active, weights[starts[4] : starts[5]])).astype(jnp.bfloat16)
    return (result, (hidden, normed, windows, context, inverse, mixed, second, upper, active))


def swin_backward(hidden_in, order, weights, gain_rows, grad_out):
    starts = block_starts()
    _, saved = swin_forward(hidden_in, order, weights, gain_rows)
    hidden, normed, windows, context, inverse, mixed, second, upper, active = saved
    grad_active = matmul_nt(grad_out, weights[starts[4] : starts[5]])
    grad_down = matmul_tn(active, grad_out)
    _, gelu_pull = jax.vjp(jax.nn.gelu, upper)
    grad_upper = gelu_pull(grad_active)[0].astype(jnp.bfloat16)
    grad_second = matmul(grad_upper, weights[starts[3] : starts[4]])
    grad_up = matmul_tn(grad_upper, second)
    back_mid, grad_gain_one = norm_back(mixed, gain_rows[1], grad_second)
    grad_mixed = grad_out.astype(jnp.float32) + back_mid
    grad_branch = grad_mixed.astype(jnp.bfloat16)[order]
    grad_context = matmul_nt(grad_branch, weights[starts[2] : starts[3]]).astype(jnp.bfloat16)
    grad_output = matmul_tn(context, grad_branch)
    grad_stack = attend_backward(
        windows[:, :, 0],
        windows[:, :, 1],
        windows[:, :, 2],
        grad_context.reshape(-1, WSZ, HEADS, HD),
    )
    grad_triple = grad_stack.reshape(-1, 3 * D)[inverse].astype(jnp.bfloat16)
    grad_normed = matmul(grad_triple, weights[starts[1] : starts[2]])
    grad_input_w = matmul_tn(grad_triple, normed)
    back_in, grad_gain_zero = norm_back(hidden, gain_rows[0], grad_normed)
    grad_in = (grad_mixed + back_in).astype(jnp.bfloat16)
    block_grad = jnp.concatenate([grad_input_w, grad_output, grad_up, grad_down], axis=0)
    return (grad_in, block_grad, jnp.stack([grad_gain_zero, grad_gain_one]))


def column_forward(hidden_in, weights, gain_rows):
    starts = block_starts()
    hidden = hidden_in.astype(jnp.float32)
    normed = layer_norm(hidden, gain_rows[2]).astype(jnp.bfloat16)
    triple = matmul_nt(normed, weights[starts[5] : starts[6]]).astype(jnp.bfloat16)
    groups = jnp.swapaxes(triple.reshape(LEV, -1, 3, HEADS, HD), 0, 1)
    context = jnp.swapaxes(
        attend_forward(groups[:, :, 0], groups[:, :, 1], groups[:, :, 2]), 0, 1
    ).reshape(-1, D)
    result = (hidden + matmul(context, weights[starts[6] : starts[7]])).astype(jnp.bfloat16)
    return (result, (hidden, normed, groups, context))


def column_backward(hidden_in, weights, gain_rows, grad_out):
    starts = block_starts()
    _, saved = column_forward(hidden_in, weights, gain_rows)
    hidden, normed, groups, context = saved
    grad_context = matmul_nt(grad_out, weights[starts[6] : starts[7]]).astype(jnp.bfloat16)
    grad_output = matmul_tn(context, grad_out)
    grad_split = jnp.swapaxes(grad_context.reshape(LEV, -1, HEADS, HD), 0, 1)
    grad_stack = attend_backward(groups[:, :, 0], groups[:, :, 1], groups[:, :, 2], grad_split)
    grad_triple = jnp.swapaxes(grad_stack, 0, 1).reshape(-1, 3 * D).astype(jnp.bfloat16)
    grad_normed = matmul(grad_triple, weights[starts[5] : starts[6]])
    grad_input_w = matmul_tn(grad_triple, normed)
    back_in, grad_gain = norm_back(hidden, gain_rows[2], grad_normed)
    grad_in = (grad_out.astype(jnp.float32) + back_in).astype(jnp.bfloat16)
    return (grad_in, jnp.concatenate([grad_input_w, grad_output], axis=0), grad_gain)


def decoder_backward(hidden_in, velocity, token_weight, weights, gain_rows, inverse_total):
    starts = block_starts()
    hidden = hidden_in.astype(jnp.float32)
    normed = layer_norm(hidden, gain_rows[3]).astype(jnp.bfloat16)
    predict = matmul_nt(normed, weights[starts[7] : starts[8]])
    error = predict - velocity
    loss_part = jnp.sum(token_weight[:, None] * error * error) * inverse_total
    grad_predict = (2.0 * inverse_total * token_weight[:, None] * error).astype(jnp.bfloat16)
    grad_decoder = matmul_tn(grad_predict, normed)
    back_in, grad_gain = norm_back(
        hidden, gain_rows[3], matmul(grad_predict, weights[starts[7] : starts[8]])
    )
    return (back_in.astype(jnp.bfloat16), grad_decoder, grad_gain, loss_part)


def adam_update(param, grad, first, second, average, correction, decay_rate, rate):
    first_new = BETA * first + (1.0 - BETA) * grad
    second_new = BETA * second + (1.0 - BETA) * grad * grad
    direction = first_new / correction / (jnp.sqrt(second_new / correction) + EPS_ADAM)
    param_new = param - rate * (direction + decay_rate * param)
    average_new = EMA_RATE * average + (1.0 - EMA_RATE) * param_new
    return (param_new, first_new, second_new, average_new)


def local(
    noise_draw,
    single_step,
    double_step,
    state_now,
    target_flag,
    flow_time,
    live_count,
    latitude_row,
    window_order,
    latitude_weight,
    level_weight,
    step_count,
    master_weights,
    first_moment,
    second_moment,
    average_weights,
    gain_rows,
    gain_first,
    gain_second,
    gain_average,
):
    micro = noise_draw.shape[0]
    tokens = noise_draw.shape[1]
    starts = block_starts()
    section = lax.axis_index("pipe")
    sections = lax.axis_size("pipe")
    members = lax.axis_size("dp")
    gathered = lax.all_gather(master_weights.astype(jnp.bfloat16), "dp", axis=0, tiled=True)
    weights = natural_order(gathered, members)
    lat_match = latitude_row[:, :, None] == jnp.arange(LATN, dtype=jnp.int32)[None, None, :]
    lat_values = jnp.sum(
        jnp.where(lat_match, latitude_weight.astype(jnp.float32)[None, None, :], 0.0), axis=2
    )
    token_weight = (
        level_weight.astype(jnp.float32)[None, :, None] * lat_values[:, None, :]
    ).reshape(micro, tokens) * 1e-06
    alive = jnp.arange(tokens, dtype=jnp.int32)[None, :] < live_count
    token_weight = jnp.where(alive, token_weight, 0.0)
    total = lax.psum(jnp.sum(token_weight), "dp")
    inverse_total = 1.0 / (PIN * total)
    zero_act = jnp.zeros((tokens, D), jnp.bfloat16)

    def encoder_inputs(slot):
        noise = noise_draw[slot].astype(jnp.float32)
        target = jnp.where(
            target_flag[slot, 0] > 0,
            double_step[slot].astype(jnp.float32),
            single_step[slot].astype(jnp.float32),
        )
        ftime = flow_time[slot, 0]
        noisy = (1.0 - ftime) * noise + ftime * target
        joined = jnp.concatenate([noisy.astype(jnp.bfloat16), state_now[slot]], axis=1)
        return (joined, target - noise)

    def encode_branch(received, stash, slot):
        joined, _ = encoder_inputs(slot)
        return (
            matmul(joined, weights[starts[0] : starts[1]]) + flow_time[slot, 0] * gain_rows[4]
        ).astype(jnp.bfloat16)

    def swin_branch(received, stash, slot):
        return swin_forward(received, window_order[slot], weights, gain_rows)[0]

    def column_branch(received, stash, slot):
        return column_forward(received, weights, gain_rows)[0]

    def quiet_branch(received, stash, slot):
        return zero_act

    def forward_tick(tick, carry):
        received, stash = carry
        number = tick - section
        valid = (number >= 0) & (number < micro)
        slot = jnp.clip(number, 0, micro - 1)
        stash = stash.at[slot].set(jnp.where(valid & (section > 0), received, stash[slot]))
        branch_index = jnp.where(valid, section, 3)
        outgoing = lax.switch(
            branch_index,
            [encode_branch, swin_branch, column_branch, quiet_branch],
            received,
            stash,
            slot,
        )
        received = jax.tree.map(
            lambda part, own: part.astype(own.dtype),
            passed_along(as_sent(outgoing), "pipe", 1),
            outgoing,
        )
        return (received, stash)

    stash_init = jnp.zeros((micro, tokens, D), jnp.bfloat16)
    _, stash = lax.fori_loop(0, micro + sections - 1, forward_tick, (zero_act, stash_init))

    def encode_back(received, slot, grads, gain_grads, loss_sum):
        joined, _ = encoder_inputs(slot)
        grads = grads.at[starts[0] : starts[1]].add(matmul_tn(joined, received))
        gain_grads = gain_grads.at[4].add(
            flow_time[slot, 0] * jnp.sum(received.astype(jnp.float32), axis=0)
        )
        return (zero_act, grads, gain_grads, loss_sum)

    def swin_back(received, slot, grads, gain_grads, loss_sum):
        grad_in, block_grad, gain_part = swin_backward(
            stash[slot], window_order[slot], weights, gain_rows, received
        )
        grads = grads.at[starts[1] : starts[5]].add(block_grad)
        gain_grads = gain_grads.at[0:2].add(gain_part)
        return (grad_in, grads, gain_grads, loss_sum)

    def column_back(received, slot, grads, gain_grads, loss_sum):
        grad_in, block_grad, gain_part = column_backward(stash[slot], weights, gain_rows, received)
        grads = grads.at[starts[5] : starts[7]].add(block_grad)
        gain_grads = gain_grads.at[2].add(gain_part)
        return (grad_in, grads, gain_grads, loss_sum)

    def decode_back(received, slot, grads, gain_grads, loss_sum):
        _, velocity = encoder_inputs(slot)
        grad_in, block_grad, gain_part, loss_part = decoder_backward(
            stash[slot], velocity, token_weight[slot], weights, gain_rows, inverse_total
        )
        grads = grads.at[starts[7] : starts[8]].add(block_grad)
        gain_grads = gain_grads.at[3].add(gain_part)
        return (grad_in, grads, gain_grads, loss_sum + loss_part)

    def quiet_back(received, slot, grads, gain_grads, loss_sum):
        return (zero_act, grads, gain_grads, loss_sum)

    def backward_tick(tick, carry):
        received, grads, gain_grads, loss_sum = carry
        number = tick - (sections - 1 - section)
        valid = (number >= 0) & (number < micro)
        slot = jnp.clip(number, 0, micro - 1)
        branch_index = jnp.where(valid, section, 4)
        outgoing, grads, gain_grads, loss_sum = lax.switch(
            branch_index,
            [encode_back, swin_back, column_back, decode_back, quiet_back],
            received,
            slot,
            grads,
            gain_grads,
            loss_sum,
        )
        received = jax.tree.map(
            lambda part, own: part.astype(own.dtype),
            passed_along(as_sent(outgoing), "pipe", -1),
            outgoing,
        )
        return (received, grads, gain_grads, loss_sum)

    grads_init = jnp.zeros((starts[8], D), jnp.float32)
    gains_init = jnp.zeros((5, D), jnp.float32)
    _, grads, gain_grads, loss_sum = lax.fori_loop(
        0,
        micro + sections - 1,
        backward_tick,
        (zero_act, grads_init, gains_init, jnp.zeros((), jnp.float32)),
    )
    grads = stored_order(grads, members)
    shard_rows = master_weights.shape[0]
    summed, gain_total, loss_total = lax.psum((grads, gain_grads, loss_sum), ("dp", "pipe"))
    square_total = jnp.sum(summed * summed)
    shard = lax.dynamic_slice_in_dim(summed, lax.axis_index("dp") * shard_rows, shard_rows, 0)
    grad_norm = jnp.sqrt(square_total + jnp.sum(gain_total * gain_total))
    factor = jnp.minimum(1.0, CLIP_MAX / (grad_norm + 1e-06))
    correction = 1.0 - jnp.power(0.5, step_count[0].astype(jnp.float32))
    new_weights, new_first, new_second, new_average = adam_update(
        master_weights,
        factor * shard,
        first_moment,
        second_moment,
        average_weights,
        correction,
        DECAY_WEIGHT,
        RATE,
    )
    new_gains, new_gain_first, new_gain_second, new_gain_average = adam_update(
        gain_rows,
        factor * gain_total,
        gain_first,
        gain_second,
        gain_average,
        correction,
        0.0,
        GAIN_RATE,
    )
    return (
        loss_total,
        grad_norm,
        new_weights,
        new_first,
        new_second,
        new_average,
        new_weights.astype(jnp.bfloat16),
        new_gains,
        new_gain_first,
        new_gain_second,
        new_gain_average,
    )


def solution(mesh):
    in_specs = (
        P(None, "dp", None),
        P(None, "dp", None),
        P(None, "dp", None),
        P(None, "dp", None),
        P(None, "dp"),
        P(None, "dp"),
        P(None, "dp"),
        P(None, "dp"),
        P(None, "dp"),
        P(),
        P(),
        P(),
        P("dp", None),
        P("dp", None),
        P("dp", None),
        P("dp", None),
        P(),
        P(),
        P(),
        P(),
    )
    out_specs = (
        P(),
        P(),
        P("dp", None),
        P("dp", None),
        P("dp", None),
        P("dp", None),
        P("dp", None),
        P(),
        P(),
        P(),
        P(),
    )
    return jax.shard_map(local, mesh=mesh, in_specs=in_specs, out_specs=out_specs, check_vma=False)
```

profile of v0, /device:TPU:0, one launch (start us, length us, event | category | flops | bytes accessed | tf_op | source)
XLA Modules:
  0.0 2019.8 jit_solution(16322665274406049566)
XLA Ops:
  13.6 24.1 %psum.28 = f32[]{:T(128)} all-reduce(f32[]{:T(128)} %fusion.197), channel_id=1, replica_groups=mesh['dp'=8,'pipe'=4] {'dp'}, use_global_device_ids=true, to_apply=%region_20.21 | all-reduce | flops 1 | bytes 8 | tf_op jit(solution)/shard_map/psum | solution.py:279
  39.2 58.0 %all-gather.2.cloned.1.call-done = bf16[6528,384]{1,0:T(8,128)(2,1)} async-done(((bf16[816,384]{1,0:T(8,128)(2,1)}), bf16[6528,384]{1,0:T(8,128)(2,1)}) %all-gather.2.cloned.1.call-update) | async-done | bytes 5013520 | tf_op jit(solution)/shard_map/all_gather | solution.py:268
  102.2 2.8 fusion.220
  105.0 3.3 fusion.221
  110.2 521.5 %while.46 = (s32[]{:T(128)}, bf16[1872,384]{1,0:T(8,128)(2,1)S(1)}, bf16[2,1872,384]{2,1,0:T(8,128)(2,1)}, s32[]{:T(128)}, f32[2,1]{0,1:T(1,128)}, /*index=5*/bf...) while((s32[]{:T(128)}, bf16[1872,384]{1,0:T(8,128)(2,1)S(1)}, ...), condition=%wide.region_17.18_spmd, body=%wide.region_0.17_spmd.sunk | while | flops 7109426176 | bytes 193363056 | solution.py:332
  111.8 21.8 %conditional.5 = (bf16[1872,384]{1,0:T(8,128)(2,1)}) conditional(s32[]{:T(128)} %clamp.29, (s32[]{:T(128)}, f32[2,1]{0,1:T(1,128)}, bf16[2,1872,128]{2,1,0:T(8,128)(2,1)}, s32[2,1]{0,1:T(1,128)}, bf16[2,1872,128]{2,1,0:T(8,128)(2,1)}, /*index=5*/bf16[2,1872,128]{2,1,0:T(8,128)(2,1)}, bf16[2,1872,128]{2,1,0:T(8,128)(2,1)}, ...), branch_computations={%region_1.1_spmd, %region_2.9_spmd, %region_10.14_spmd, %region_15... | conditional | flops 7107988480 | bytes 166045120 | solution.py:317
  115.6 2.8 fusion.12
  119.4 2.7 fusion.8
  141.1 10.5 conditional.5
  144.9 2.8 fusion.12
  151.6 141.1 %collective-permute-start = (bf16[1872,384]{1,0:T(8,128)(2,1)}, bf16[1872,384]{1,0:T(8,128)(2,1)S(1)}, u32[]{:S(2)}, u32[]{:S(2)}) collective-permute-start(bf16[1872,384]{1,0:T(8,128)(2,1)} %get-tuple-element.1986), channel_id=1, source_target_pairs={{0,1},{1,2},{2,3},{4,5},{5,6},{6,7},{8,9},{9,10},{10,11},{12,13},{... | collective-permute-start | bytes 4313096 | tf_op jit(solution)/shard_map/while/body/eval_jaxpr/ppermute | solution.py:37
  299.9 151.4 %collective-permute-start = (bf16[1872,384]{1,0:T(8,128)(2,1)}, bf16[1872,384]{1,0:T(8,128)(2,1)S(1)}, u32[]{:S(2)}, u32[]{:S(2)}) collective-permute-start(bf16[1872,384]{1,0:T(8,128)(2,1)} %get-tuple-element.1986), channel_id=1, source_target_pairs={{0,1},{1,2},{2,3},{4,5},{5,6},{6,7},{8,9},{9,10},{10,11},{12,13},{... | collective-permute-start | bytes 4313096 | tf_op jit(solution)/shard_map/while/body/eval_jaxpr/ppermute | solution.py:37
  458.5 30.6 %collective-permute-start = (bf16[1872,384]{1,0:T(8,128)(2,1)}, bf16[1872,384]{1,0:T(8,128)(2,1)S(1)}, u32[]{:S(2)}, u32[]{:S(2)}) collective-permute-start(bf16[1872,384]{1,0:T(8,128)(2,1)} %get-tuple-element.1986), channel_id=1, source_target_pairs={{0,1},{1,2},{2,3},{4,5},{5,6},{6,7},{8,9},{9,10},{10,11},{12,13},{... | collective-permute-start | bytes 4313096 | tf_op jit(solution)/shard_map/while/body/eval_jaxpr/ppermute | solution.py:37
  496.3 129.2 %collective-permute-start = (bf16[1872,384]{1,0:T(8,128)(2,1)}, bf16[1872,384]{1,0:T(8,128)(2,1)S(1)}, u32[]{:S(2)}, u32[]{:S(2)}) collective-permute-start(bf16[1872,384]{1,0:T(8,128)(2,1)} %get-tuple-element.1986), channel_id=1, source_target_pairs={{0,1},{1,2},{2,3},{4,5},{5,6},{6,7},{8,9},{9,10},{10,11},{12,13},{... | collective-permute-start | bytes 4313096 | tf_op jit(solution)/shard_map/while/body/eval_jaxpr/ppermute | solution.py:37
  632.3 4.4 broadcast_in_dim.70
  636.8 1130.3 %while.47 = (s32[]{:T(128)}, bf16[1872,384]{1,0:T(8,128)(2,1)S(1)}, f32[6528,384]{1,0:T(8,128)}, f32[5,384]{1,0:T(8,128)}, f32[]{:T(128)}, /*index=5*/s32[]{:T(1...) while((s32[]{:T(128)}, bf16[1872,384]{1,0:T(8,128)(2,1)S(1)}, ...), condition=%wide.region_56.57_spmd.clone, body=%wide.region_21.56_spmd.clone.sunk | while | flops 19110486016 | bytes 587465984 | solution.py:392
  637.4 29.2 %conditional.6 = (bf16[1872,384]{1,0:T(8,128)(2,1)}, f32[6528,384]{1,0:T(8,128)}, f32[5,384]{1,0:T(8,128)}, f32[]{:T(128)}) conditional(s32[]{:T(128)} %clamp.30, (f32[6528,384]{1,0:T(8,128)}, s32[]{:T(128)}, f32[2,1]{0,1:T(1,128)}, bf16[2,1872,128]{2,1,0:T(8,128)(2,1)}, s32[2,1]{0,1:T(1,128)}, ...), branch_computations={%region_22.23_spmd, %region_24.38_spmd, %region_39.47_spmd, %regio... | conditional | flops 19110486016 | bytes 581699456 | solution.py:374
  667.8 34.7 %collective-permute-done.1 = bf16[1872,384]{1,0:T(8,128)(2,1)S(1)} collective-permute-done((bf16[1872,384]{1,0:T(8,128)(2,1)}, bf16[1872,384]{1,0:T(8,128)(2,1)S(1)}, u32[]{:S(2)}, u32[]{:S(2)}) %collective-permute-start.1) | collective-permute-done | bytes 1437728 | tf_op jit(solution)/shard_map/while/body/eval_jaxpr/ppermute | solution.py:37
  702.8 29.3 %conditional.6 = (bf16[1872,384]{1,0:T(8,128)(2,1)}, f32[6528,384]{1,0:T(8,128)}, f32[5,384]{1,0:T(8,128)}, f32[]{:T(128)}) conditional(s32[]{:T(128)} %clamp.30, (f32[6528,384]{1,0:T(8,128)}, s32[]{:T(128)}, f32[2,1]{0,1:T(1,128)}, bf16[2,1872,128]{2,1,0:T(8,128)(2,1)}, s32[2,1]{0,1:T(1,128)}, ...), branch_computations={%region_22.23_spmd, %region_24.38_spmd, %region_39.47_spmd, %regio... | conditional | flops 19110486016 | bytes 581699456 | solution.py:374
  733.4 20.0 collective-permute-done.1
  753.7 21.4 %conditional.6 = (bf16[1872,384]{1,0:T(8,128)(2,1)}, f32[6528,384]{1,0:T(8,128)}, f32[5,384]{1,0:T(8,128)}, f32[]{:T(128)}) conditional(s32[]{:T(128)} %clamp.30, (f32[6528,384]{1,0:T(8,128)}, s32[]{:T(128)}, f32[2,1]{0,1:T(1,128)}, bf16[2,1872,128]{2,1,0:T(8,128)(2,1)}, s32[2,1]{0,1:T(1,128)}, ...), branch_computations={%region_22.23_spmd, %region_24.38_spmd, %region_39.47_spmd, %regio... | conditional | flops 19110486016 | bytes 581699456 | solution.py:374
  776.5 592.4 %collective-permute-done.1 = bf16[1872,384]{1,0:T(8,128)(2,1)S(1)} collective-permute-done((bf16[1872,384]{1,0:T(8,128)(2,1)}, bf16[1872,384]{1,0:T(8,128)(2,1)S(1)}, u32[]{:S(2)}, u32[]{:S(2)}) %collective-permute-start.1) | collective-permute-done | bytes 1437728 | tf_op jit(solution)/shard_map/while/body/eval_jaxpr/ppermute | solution.py:37
  1369.5 31.7 %conditional.6 = (bf16[1872,384]{1,0:T(8,128)(2,1)}, f32[6528,384]{1,0:T(8,128)}, f32[5,384]{1,0:T(8,128)}, f32[]{:T(128)}) conditional(s32[]{:T(128)} %clamp.30, (f32[6528,384]{1,0:T(8,128)}, s32[]{:T(128)}, f32[2,1]{0,1:T(1,128)}, bf16[2,1872,128]{2,1,0:T(8,128)(2,1)}, s32[2,1]{0,1:T(1,128)}, ...), branch_computations={%region_22.23_spmd, %region_24.38_spmd, %region_39.47_spmd, %regio... | conditional | flops 19110486016 | bytes 581699456 | solution.py:374
  1375.6 2.9 fusion.6
  1402.5 317.9 %collective-permute-done.1 = bf16[1872,384]{1,0:T(8,128)(2,1)S(1)} collective-permute-done((bf16[1872,384]{1,0:T(8,128)(2,1)}, bf16[1872,384]{1,0:T(8,128)(2,1)S(1)}, u32[]{:S(2)}, u32[]{:S(2)}) %collective-permute-start.1) | collective-permute-done | bytes 1437728 | tf_op jit(solution)/shard_map/while/body/eval_jaxpr/ppermute | solution.py:37
  1720.6 31.8 %conditional.6 = (bf16[1872,384]{1,0:T(8,128)(2,1)}, f32[6528,384]{1,0:T(8,128)}, f32[5,384]{1,0:T(8,128)}, f32[]{:T(128)}) conditional(s32[]{:T(128)} %clamp.30, (f32[6528,384]{1,0:T(8,128)}, s32[]{:T(128)}, f32[2,1]{0,1:T(1,128)}, bf16[2,1872,128]{2,1,0:T(8,128)(2,1)}, s32[2,1]{0,1:T(1,128)}, ...), branch_computations={%region_22.23_spmd, %region_24.38_spmd, %region_39.47_spmd, %regio... | conditional | flops 19110486016 | bytes 581699456 | solution.py:374
  1726.8 2.9 fusion.6
  1753.7 8.9 collective-permute-done.1
  1785.1 55.7 %all-reduce = (f32[]{:T(128)}, f32[5,384]{1,0:T(8,128)S(1)}) all-reduce(f32[]{:T(128)} %get-tuple-element.1227, f32[5,384]{1,0:T(8,128)} %get-tuple-element.1229), channel_id=1, replica_groups=mesh['dp'=8,'pipe'=4] {'dp','pipe'}, use_global_device_ids=true, to_apply=%region_57.58 | all-reduce | flops 1921 | bytes 15368 | tf_op jit(solution)/shard_map/psum | solution.py:400
  1841.4 155.3 %all-reduce.3.cloned.1.call-done = f32[6528,384]{1,0:T(8,128)} async-done(((f32[6528,384]{1,0:T(8,128)}), f32[6528,384]{1,0:T(8,128)}) %all-reduce.3.cloned.1.call-update) | async-done | bytes 10027024 | tf_op jit(solution)/shard_map/psum | solution.py:400
  1996.8 7.0 multiply_reduce_fusion.11
  2005.2 4.2 fusion.205
  (155 shorter events, 114.4 us)
Async XLA Ops:
  7.2 90.0 %all-gather.2.cloned.1.call-start = ((), (), s32[]{:S(2)}) async-start(), calls=%async_computation | async-start | bytes 5640192 | tf_op jit(solution)/shard_map/all_gather | solution.py:268
  9.4 1987.3 %all-reduce.3.cloned.1.call-start = ((), (), s32[]{:S(2)}) async-start(), calls=%async_computation.1 | async-start | bytes 20054016 | tf_op jit(solution)/shard_map/psum | solution.py:400
  108.3 1.9 copy-start.51
  110.6 1.2 copy-start
  110.6 24.5 %copy-start.58 = (s32[3]{0:T(128)S(1)}, s32[3]{0:T(128)}, u32[]{:S(2)}) copy-start(s32[3]{0:T(128)} %get-tuple-element.1891) | copy-start | bytes 40 | tf_op jit(solution)/shard_map/while
  133.6 3.8 copy-start.1
  133.6 6.0 collective-permute-start
  139.9 1.2 copy-start
  140.0 152.7 %copy-start.58 = (s32[3]{0:T(128)S(1)}, s32[3]{0:T(128)}, u32[]{:S(2)}) copy-start(s32[3]{0:T(128)} %get-tuple-element.1891) | copy-start | bytes 40 | tf_op jit(solution)/shard_map/while
  151.6 143.3 %copy-start.1 = (bf16[1872,384]{1,0:T(8,128)(2,1)S(1)}, bf16[1872,384]{1,0:T(8,128)(2,1)}, u32[]{:S(2)}) copy-start(bf16[1872,384]{1,0:T(8,128)(2,1)} %copy-done) | copy-start | bytes 4313092 | tf_op jit(solution)/shard_map/while
  151.6 145.5 %collective-permute-start = (bf16[1872,384]{1,0:T(8,128)(2,1)}, bf16[1872,384]{1,0:T(8,128)(2,1)S(1)}, u32[]{:S(2)}, u32[]{:S(2)}) collective-permute-start(bf16[1872,384]{1,0:T(8,128)(2,1)} %get-tuple-element.1986), channel_id=1, source_target_pairs={{0,1},{1,2},{2,3},{4,5},{5,6},{6,7},{8,9},{9,10},{10,11},{12,13},{... | collective-permute-start | bytes 4313096 | tf_op jit(solution)/shard_map/while/body/eval_jaxpr/ppermute | solution.py:37
  297.5 153.8 %copy-start.58 = (s32[3]{0:T(128)S(1)}, s32[3]{0:T(128)}, u32[]{:S(2)}) copy-start(s32[3]{0:T(128)} %get-tuple-element.1891) | copy-start | bytes 40 | tf_op jit(solution)/shard_map/while
  299.9 153.6 %copy-start.1 = (bf16[1872,384]{1,0:T(8,128)(2,1)S(1)}, bf16[1872,384]{1,0:T(8,128)(2,1)}, u32[]{:S(2)}) copy-start(bf16[1872,384]{1,0:T(8,128)(2,1)} %copy-done) | copy-start | bytes 4313092 | tf_op jit(solution)/shard_map/while
  299.9 155.9 %collective-permute-start = (bf16[1872,384]{1,0:T(8,128)(2,1)}, bf16[1872,384]{1,0:T(8,128)(2,1)S(1)}, u32[]{:S(2)}, u32[]{:S(2)}) collective-permute-start(bf16[1872,384]{1,0:T(8,128)(2,1)} %get-tuple-element.1986), channel_id=1, source_target_pairs={{0,1},{1,2},{2,3},{4,5},{5,6},{6,7},{8,9},{9,10},{10,11},{12,13},{... | collective-permute-start | bytes 4313096 | tf_op jit(solution)/shard_map/while/body/eval_jaxpr/ppermute | solution.py:37
  456.1 33.0 %copy-start.58 = (s32[3]{0:T(128)S(1)}, s32[3]{0:T(128)}, u32[]{:S(2)}) copy-start(s32[3]{0:T(128)} %get-tuple-element.1891) | copy-start | bytes 40 | tf_op jit(solution)/shard_map/while
  458.5 32.9 %copy-start.1 = (bf16[1872,384]{1,0:T(8,128)(2,1)S(1)}, bf16[1872,384]{1,0:T(8,128)(2,1)}, u32[]{:S(2)}) copy-start(bf16[1872,384]{1,0:T(8,128)(2,1)} %copy-done) | copy-start | bytes 4313092 | tf_op jit(solution)/shard_map/while
  458.5 35.1 %collective-permute-start = (bf16[1872,384]{1,0:T(8,128)(2,1)}, bf16[1872,384]{1,0:T(8,128)(2,1)S(1)}, u32[]{:S(2)}, u32[]{:S(2)}) collective-permute-start(bf16[1872,384]{1,0:T(8,128)(2,1)} %get-tuple-element.1986), channel_id=1, source_target_pairs={{0,1},{1,2},{2,3},{4,5},{5,6},{6,7},{8,9},{9,10},{10,11},{12,13},{... | collective-permute-start | bytes 4313096 | tf_op jit(solution)/shard_map/while/body/eval_jaxpr/ppermute | solution.py:37
  493.9 131.5 %copy-start.58 = (s32[3]{0:T(128)S(1)}, s32[3]{0:T(128)}, u32[]{:S(2)}) copy-start(s32[3]{0:T(128)} %get-tuple-element.1891) | copy-start | bytes 40 | tf_op jit(solution)/shard_map/while
  496.3 131.4 %copy-start.1 = (bf16[1872,384]{1,0:T(8,128)(2,1)S(1)}, bf16[1872,384]{1,0:T(8,128)(2,1)}, u32[]{:S(2)}) copy-start(bf16[1872,384]{1,0:T(8,128)(2,1)} %copy-done) | copy-start | bytes 4313092 | tf_op jit(solution)/shard_map/while
  496.3 133.6 %collective-permute-start = (bf16[1872,384]{1,0:T(8,128)(2,1)}, bf16[1872,384]{1,0:T(8,128)(2,1)S(1)}, u32[]{:S(2)}, u32[]{:S(2)}) collective-permute-start(bf16[1872,384]{1,0:T(8,128)(2,1)} %get-tuple-element.1986), channel_id=1, source_target_pairs={{0,1},{1,2},{2,3},{4,5},{5,6},{6,7},{8,9},{9,10},{10,11},{12,13},{... | collective-permute-start | bytes 4313096 | tf_op jit(solution)/shard_map/while/body/eval_jaxpr/ppermute | solution.py:37
  666.5 36.0 %collective-permute-start.1 = (bf16[1872,384]{1,0:T(8,128)(2,1)}, bf16[1872,384]{1,0:T(8,128)(2,1)S(1)}, u32[]{:S(2)}, u32[]{:S(2)}) collective-permute-start(bf16[1872,384]{1,0:T(8,128)(2,1)} %get-tuple-element.1791), channel_id=1, source_target_pairs={{1,0},{2,1},{3,2},{5,4},{6,5},{7,6},{9,8},{10,9},{11,10},{13,12},{... | collective-permute-start | bytes 4313096 | tf_op jit(solution)/shard_map/while/body/eval_jaxpr/ppermute | solution.py:37
  732.1 21.3 %collective-permute-start.1 = (bf16[1872,384]{1,0:T(8,128)(2,1)}, bf16[1872,384]{1,0:T(8,128)(2,1)S(1)}, u32[]{:S(2)}, u32[]{:S(2)}) collective-permute-start(bf16[1872,384]{1,0:T(8,128)(2,1)} %get-tuple-element.1791), channel_id=1, source_target_pairs={{1,0},{2,1},{3,2},{5,4},{6,5},{7,6},{9,8},{10,9},{11,10},{13,12},{... | collective-permute-start | bytes 4313096 | tf_op jit(solution)/shard_map/while/body/eval_jaxpr/ppermute | solution.py:37
  775.2 593.7 %collective-permute-start.1 = (bf16[1872,384]{1,0:T(8,128)(2,1)}, bf16[1872,384]{1,0:T(8,128)(2,1)S(1)}, u32[]{:S(2)}, u32[]{:S(2)}) collective-permute-start(bf16[1872,384]{1,0:T(8,128)(2,1)} %get-tuple-element.1791), channel_id=1, source_target_pairs={{1,0},{2,1},{3,2},{5,4},{6,5},{7,6},{9,8},{10,9},{11,10},{13,12},{... | collective-permute-start | bytes 4313096 | tf_op jit(solution)/shard_map/while/body/eval_jaxpr/ppermute | solution.py:37
  1401.2 319.2 %collective-permute-start.1 = (bf16[1872,384]{1,0:T(8,128)(2,1)}, bf16[1872,384]{1,0:T(8,128)(2,1)S(1)}, u32[]{:S(2)}, u32[]{:S(2)}) collective-permute-start(bf16[1872,384]{1,0:T(8,128)(2,1)} %get-tuple-element.1791), channel_id=1, source_target_pairs={{1,0},{2,1},{3,2},{5,4},{6,5},{7,6},{9,8},{10,9},{11,10},{13,12},{... | collective-permute-start | bytes 4313096 | tf_op jit(solution)/shard_map/while/body/eval_jaxpr/ppermute | solution.py:37
  1752.4 10.2 collective-permute-start.1
  1841.4 163.7 %copy-start.24 = (f32[816,384]{1,0:T(8,128)S(1)}, f32[816,384]{1,0:T(8,128)}, u32[]{:S(2)}) copy-start(f32[816,384]{1,0:T(8,128)} %param.63) | copy-start | bytes 3760132
  1841.4 163.8 %copy-start.38 = (f32[816,384]{1,0:T(8,128)S(1)}, f32[816,384]{1,0:T(8,128)}, u32[]{:S(2)}) copy-start(f32[816,384]{1,0:T(8,128)} %param.65) | copy-start | bytes 3760132
  2005.2 4.2 copy-start.39
  2009.4 2.1 copy-start.25
  2009.4 1.4 copy-start.59
  2009.4 1.4 copy-start.60
  2009.4 1.5 copy-start.61
  (4 other events, 4.1 us)
Sparse Core Ops, SparseCore 0:
  10.8 86.3 all-gather.1
  1784.5 212.1 all-reduce.2
where the time goes:
time: 2030 us; the launch traced here: 2020 us
  waiting for transfers between devices  1190 us (59%)
  starting transfers between devices  460 us (23%)
  loops' own time  136 us (7%)
  blocking collectives  79.8 us (4%)
  local copies, waits for them, and re-layouts  72.8 us (4%)
  other arithmetic  55.1 us (3%)
    ppermute x10, waiting for transfers between devices, passed_along(): return lax.ppermute(value, axis, pairs)  974 us
    ppermute x10, starting transfers between devices, passed_along(): return lax.ppermute(value, axis, pairs)  460 us
    psum x1, waiting for transfers between devices, local(): lax.psum((grads, gain_grads, loss_sum), ('dp', 'pipe'))  155 us
    another operation x5, loops' own time, backward_tick(): lax.switch(branch_index, [encode_back, swin_back, column_back, decode_bac...  113 us
    all_gather x1, waiting for transfers between devices, local(): lax.all_gather(master_weights.astype(jnp.bfloat16), 'dp', axis=0, tiled=T...  58 us
    psum x1, blocking collectives, local(): lax.psum((grads, gain_grads, loss_sum), ('dp', 'pipe'))  55.7 us
  transfers between devices with their start and end apart: 12, of which 7 were waited for; matrix products, arithmetic and copies ran while one was open for 1% of the time, Pallas kernels for 0%

commit v1 on v0

v1 whole, which is shorter than its diff:
```python
import functools

import jax
import jax.numpy as jnp
import numpy as np
from jax import lax
from jax.experimental import pallas as pl
from jax.experimental.pallas import tpu as pltpu
from jax.sharding import PartitionSpec as P

D = 384
HEADS = 12
HD = 32
FF = 1536
PIN = 128
LEV = 13
WSZ = 144
LATN = 60

EPS_NORM = 1e-05
CLIP_MAX = 0.01
RATE = 0.03
GAIN_RATE = 0.3
BETA = 0.5
EPS_ADAM = 1e-08
DECAY_WEIGHT = 0.05
EMA_RATE = 0.8

F32 = jnp.float32
BF16 = jnp.bfloat16
MESH = pl.DeviceIdType.MESH

SOFT = HD ** (-0.5) * 1.4426950408889634
GROUPS = 3
PACK = 4
LANES = 128

ROWS = 1008
TILE = 336
TILES = 3
WINS = 7
CHUNKS = 9
CROWS = 112
VMEM_MAX = 60 * 2**20


def block_starts():
    widths = [2 * PIN, 3 * D, D, FF, FF, 3 * D, D, PIN]
    starts = [0]
    for width in widths:
        starts.append(starts[-1] + width)
    return starts


STARTS = block_starts()


def natural_order(stored, pieces_count):
    view = stored.reshape(pieces_count, stored.shape[0] // pieces_count, stored.shape[1])
    pieces = []
    for number in range(8):
        pieces.append(
            view[:, STARTS[number] // pieces_count : STARTS[number + 1] // pieces_count].reshape(
                -1, stored.shape[1]
            )
        )
    return jnp.concatenate(pieces, axis=0)


def stored_order(natural, pieces_count):
    pieces = []
    for number in range(8):
        pieces.append(
            natural[STARTS[number] : STARTS[number + 1]].reshape(pieces_count, -1, natural.shape[1])
        )
    return jnp.concatenate(pieces, axis=1).reshape(-1, natural.shape[1])


def dot(left, right):
    return jnp.dot(left, right, preferred_element_type=F32)


def dot_nt(left, right):
    return lax.dot_general(left, right, (((1,), (1,)), ((), ())), preferred_element_type=F32)


def dot_tn(left, right):
    return lax.dot_general(left, right, (((0,), (0,)), ((), ())), preferred_element_type=F32)


def standardize(values):
    center = values - jnp.mean(values, axis=-1, keepdims=True)
    spread = lax.rsqrt(jnp.mean(center * center, axis=-1, keepdims=True) + EPS_NORM)
    return center * spread, spread


def standardize_back(scaled, spread, gain, upstream):
    inner = upstream * gain
    return spread * (
        inner
        - jnp.mean(inner, axis=-1, keepdims=True)
        - scaled * jnp.mean(inner * scaled, axis=-1, keepdims=True)
    )


def head_masks(dtype):
    lane = lax.broadcasted_iota(jnp.int32, (1, LANES), 1) // HD
    return [jnp.where(lane == h, 1.0, 0.0).astype(dtype) for h in range(PACK)]


def spread_heads(block):
    return jnp.concatenate([block * mask for mask in head_masks(block.dtype)], axis=0)


def gather_heads(stacked, n):
    masks = head_masks(F32)
    total = stacked[0:n] * masks[0]
    for h in range(1, PACK):
        total = total + stacked[h * n : (h + 1) * n] * masks[h]
    return total


def attend(query, keys, values, keep):
    n = query.shape[0]
    scores = dot_nt(spread_heads(keys), query)
    if keep is not None:
        scores = jnp.where(keep, scores, -1e30)
    blocks = scores.reshape(PACK, n, n)
    top = jnp.max(blocks, axis=1, keepdims=True)
    expo = jnp.exp2((blocks - top) * SOFT)
    probs = expo * (1.0 / jnp.sum(expo, axis=1, keepdims=True))
    probs = probs.reshape(PACK * n, n)
    context = dot_tn(probs.astype(BF16), spread_heads(values))
    return probs, context


def attend_back(probs, query, keys, values, upstream):
    n = query.shape[0]
    probs_low = probs.astype(BF16)
    wide = probs.astype(F32).reshape(PACK, n, n)
    grad_values = gather_heads(dot(probs_low, upstream), n)
    grad_probs = dot_nt(spread_heads(values), upstream).reshape(PACK, n, n)
    delta = jnp.sum(wide * grad_probs, axis=1, keepdims=True)
    grad_scores = (wide * (grad_probs - delta)).astype(BF16).reshape(PACK * n, n)
    factor = HD ** (-0.5)
    grad_query = dot_tn(grad_scores, spread_heads(keys)) * factor
    grad_keys = gather_heads(dot(grad_scores, query), n) * factor
    return grad_query, grad_keys, grad_values


def column_of(row):
    wide = jnp.broadcast_to(row.astype(F32), (LANES, row.shape[1]))
    return jnp.transpose(wide)


def tile_at(t):
    return pl.ds(pl.multiple_of(t * TILE, 16), TILE)


def group_at(which, g):
    start = which * D + g * LANES
    return slice(start, start + LANES)


def window_forward(
    ints, floats, noise_any, single_any, double_any, state_any, order_ref, weights, gains,
    joined, h0, a_out, r1, probs, ctx1, h1, m_out, slope, y_out, h2,
    column, picks, source, raw, sems,
):
    slot = ints[0]
    flag = ints[2]
    ftime = floats[0]
    copies = [
        pltpu.make_async_copy(ref.at[slot], raw.at[i], sems.at[i])
        for i, ref in enumerate((noise_any, single_any, double_any, state_any))
    ]
    for copy in copies:
        copy.start()
    column[...] = column_of(order_ref[...]).astype(jnp.int32)
    for copy in copies:
        copy.wait()
    tokens = raw.shape[1]
    source[tokens:, :] = jnp.zeros((source.shape[0] - tokens, D), BF16)
    source[:tokens, 0:PIN] = raw[0]
    source[:tokens, PIN : 2 * PIN] = jnp.where(flag > 0, raw[2], raw[1])
    source[:tokens, 2 * PIN :] = raw[3]

    @pl.loop(0, TILES)
    def _(t):
        rows = tile_at(t)
        own = column[rows, :]
        lane = lax.broadcasted_iota(jnp.int32, (1, LANES), 1)
        for b in range(picks.shape[1] // LANES):
            picks[:, b * LANES : (b + 1) * LANES] = jnp.where(
                own == lane + b * LANES, 1.0, 0.0
            ).astype(BF16)
        drawn = dot(picks[...], source[...])
        noisy = (1.0 - ftime) * drawn[:, 0:PIN] + ftime * drawn[:, PIN : 2 * PIN]
        both = jnp.concatenate([noisy.astype(BF16), drawn[:, 2 * PIN :].astype(BF16)], axis=1)
        joined[rows, :] = both
        low = (dot(both, weights[STARTS[0] : STARTS[1], :]) + ftime * gains[4:5, :]).astype(BF16)
        h0[rows, :] = low
        scaled, _ = standardize(low.astype(F32))
        normed = (scaled * gains[0:1, :]).astype(BF16)
        a_out[rows, :] = normed
        r1[rows, :] = dot_nt(normed, weights[STARTS[1] : STARTS[2], :]).astype(BF16)

    @pl.loop(0, WINS)
    def _(w):
        rows = pl.ds(pl.multiple_of(w * WSZ, 16), WSZ)
        for g in range(GROUPS):
            p, context = attend(
                r1[rows, group_at(0, g)], r1[rows, group_at(1, g)], r1[rows, group_at(2, g)], None
            )
            probs[w * GROUPS + g] = p.astype(BF16)
            ctx1[rows, g * LANES : (g + 1) * LANES] = context.astype(BF16)

    @pl.loop(0, TILES)
    def _(t):
        rows = tile_at(t)
        mixed = h0[rows, :].astype(F32) + dot(ctx1[rows, :], weights[STARTS[2] : STARTS[3], :])
        h1[rows, :] = mixed
        scaled, _ = standardize(mixed)
        second = (scaled * gains[1:2, :]).astype(BF16)
        m_out[rows, :] = second
        upper = dot_nt(second, weights[STARTS[3] : STARTS[4], :])
        coef = 0.7978845608028654
        square = upper * upper
        bent = jnp.tanh(coef * (upper + 0.044715 * (square * upper)))
        half_up = 0.5 * (1.0 + bent)
        active = (upper * half_up).astype(BF16)
        y_out[rows, :] = active
        slope[rows, :] = half_up + 0.5 * upper * (1.0 - bent * bent) * (
            coef * (1.0 + 3 * 0.044715 * square)
        )
        h2[rows, :] = (mixed + dot(active, weights[STARTS[4] : STARTS[5], :])).astype(BF16)


def column_both(
    floats, noise_any, single_any, double_any, h2_own, order_ref, table_ref, token_ref,
    weights, gains,
    grads, small, everyone,
    column, token_w, picks, allh, velocity, raw, h2, c_s, r2, probs, ctx2, dctx, dh3_s, f_s, dpred_s, dr2,
    sems, send_sem, recv_sem,
):
    half = lax.rem(lax.axis_index("pipe"), 2)
    slot = lax.axis_index("pipe") // 2
    double = jnp.full((1, PIN), floats[2], F32) > 0.5
    scale = floats[1]
    partner = {"pipe": lax.axis_index("pipe") + 1 - 2 * half}
    barrier = pltpu.get_barrier_semaphore()
    pl.semaphore_signal(barrier, inc=1, device_id=partner, device_id_type=MESH)
    copies = [
        pltpu.make_async_copy(ref.at[slot], raw.at[i], sems.at[i])
        for i, ref in enumerate((noise_any, single_any, double_any))
    ]
    for copy in copies:
        copy.start()
    allh[pl.ds(pl.multiple_of(half * 864, 16), ROWS), :] = h2_own[...]
    allh[13 * WSZ :, :] = jnp.zeros((allh.shape[0] - 13 * WSZ, D), BF16)
    pl.semaphore_wait(barrier, 1)
    sent = allh.at[pl.ds(pl.multiple_of(half * ROWS, 16), 864), :]
    swap = pltpu.make_async_remote_copy(
        src_ref=sent, dst_ref=sent, send_sem=send_sem.at[0], recv_sem=recv_sem.at[0],
        device_id=partner, device_id_type=MESH,
    )
    swap.start()
    table = column_of(table_ref[...]).astype(jnp.int32)
    column[...] = jnp.where(table >= 0, table + 8 * half, -9)
    token_w[...] = column_of(token_ref[...])
    for copy in copies:
        copy.wait()

    @pl.loop(0, CHUNKS)
    def _(k):
        for lev in range(LEV):
            at = pl.ds(pl.multiple_of(lev * WSZ + k * 16, 16), 16)
            noise = raw[0, at, :].astype(F32)
            target = jnp.where(double, raw[2, at, :].astype(F32), raw[1, at, :].astype(F32))
            speed = target - noise
            velocity[pl.ds(pl.multiple_of(k * CROWS + lev * 8, 8), 8), :] = jnp.where(
                half > 0, speed[8:16], speed[0:8]
            )
        velocity[pl.ds(pl.multiple_of(k * CROWS + LEV * 8, 8), 8), :] = jnp.zeros((8, PIN), F32)

    swap.wait()

    @pl.loop(0, TILES)
    def _(t):
        rows = tile_at(t)
        own = column[rows, :]
        for b in range(picks.shape[1] // LANES):
            picks[:, b * LANES : (b + 1) * LANES] = jnp.where(
                own == order_ref[:, b * LANES : (b + 1) * LANES], 1.0, 0.0
            ).astype(BF16)
        hidden = dot(picks[...], allh[...])
        h2[rows, :] = hidden.astype(BF16)
        scaled, _ = standardize(hidden)
        normed = (scaled * gains[2:3, :]).astype(BF16)
        c_s[rows, :] = normed
        r2[rows, :] = dot_nt(normed, weights[0 : 3 * D, :]).astype(BF16)

    def same_column():
        key = lax.broadcasted_iota(jnp.int32, (PACK, CROWS, CROWS), 1)
        ask = lax.broadcasted_iota(jnp.int32, (PACK, CROWS, CROWS), 2)
        keep = (lax.bitwise_and(key, 7) == lax.bitwise_and(ask, 7)) & (key < LEV * 8)
        return keep.reshape(PACK * CROWS, CROWS)

    @pl.loop(0, CHUNKS)
    def _(k):
        rows = pl.ds(pl.multiple_of(k * CROWS, 16), CROWS)
        keep = same_column()
        for g in range(GROUPS):
            p, context = attend(
                r2[rows, group_at(0, g)], r2[rows, group_at(1, g)], r2[rows, group_at(2, g)], keep
            )
            probs[k * GROUPS + g] = p.astype(probs.dtype)
            ctx2[rows, g * LANES : (g + 1) * LANES] = context.astype(BF16)

    small[...] = jnp.zeros_like(small)

    @pl.loop(0, TILES)
    def _(t):
        rows = tile_at(t)
        o2 = weights[3 * D : 4 * D, :]
        deq = weights[4 * D :, :]
        hidden = (h2[rows, :].astype(F32) + dot(ctx2[rows, :], o2)).astype(BF16).astype(F32)
        scaled, spread = standardize(hidden)
        normed = (scaled * gains[3:4, :]).astype(BF16)
        f_s[rows, :] = normed
        error = dot_nt(normed, deq) - velocity[rows, :]
        weighed = token_w[rows, :] * error
        small[2:3, 0:PIN] += jnp.sum(weighed * error, axis=0, keepdims=True) * scale
        dpred = (2.0 * scale * weighed).astype(BF16)
        dpred_s[rows, :] = dpred
        upstream = dot(dpred, deq)
        small[1:2, :] += jnp.sum(upstream * scaled, axis=0, keepdims=True)
        dh3 = standardize_back(scaled, spread, gains[3:4, :], upstream).astype(BF16)
        dh3_s[rows, :] = dh3
        dctx[rows, :] = dot_nt(dh3, o2).astype(BF16)

    grads[4 * D :, :] = dot_tn(dpred_s[...], f_s[...])
    grads[3 * D : 4 * D, :] = dot_tn(ctx2[...], dh3_s[...])

    @pl.loop(0, CHUNKS)
    def _(k):
        rows = pl.ds(pl.multiple_of(k * CROWS, 16), CROWS)
        for g in range(GROUPS):
            parts = attend_back(
                probs[k * GROUPS + g],
                r2[rows, group_at(0, g)],
                r2[rows, group_at(1, g)],
                r2[rows, group_at(2, g)],
                dctx[rows, g * LANES : (g + 1) * LANES],
            )
            for i, part in enumerate(parts):
                dr2[rows, group_at(i, g)] = part.astype(BF16)

    base = pl.multiple_of(half * ROWS, 16)

    @pl.loop(0, TILES)
    def _(t):
        rows = tile_at(t)
        upstream = dot(dr2[rows, :], weights[0 : 3 * D, :])
        scaled, spread = standardize(h2[rows, :].astype(F32))
        small[0:1, :] += jnp.sum(upstream * scaled, axis=0, keepdims=True)
        back = standardize_back(scaled, spread, gains[2:3, :], upstream)
        everyone[pl.ds(pl.multiple_of(base + t * TILE, 16), TILE), :] = (
            dh3_s[rows, :].astype(F32) + back
        ).astype(BF16)

    everyone[2 * ROWS :, :] = jnp.zeros((everyone.shape[0] - 2 * ROWS, D), BF16)
    out = everyone.at[pl.ds(base, ROWS), :]
    swap_back = pltpu.make_async_remote_copy(
        src_ref=out, dst_ref=out, send_sem=send_sem.at[1], recv_sem=recv_sem.at[1],
        device_id=partner, device_id_type=MESH,
    )
    swap_back.start()
    for i in range(3):
        grads[i * D : (i + 1) * D, :] = dot_tn(dr2[:, i * D : (i + 1) * D], c_s[...])
    swap_back.wait()


def window_backward(
    floats, everyone, order_ref, table_ref, weights, gains,
    joined, h0, a_in, r1, probs, ctx1, h1, m_in, slope, y_in,
    grads, small,
    column, picks, dh2_s, du_s, dh1_s, do_s, dctx, dr1, dh0_s,
):
    ftime = floats[0]
    column[...] = column_of(order_ref[...]).astype(jnp.int32)
    small[...] = jnp.zeros_like(small)

    @pl.loop(0, TILES)
    def _(t):
        rows = tile_at(t)
        own = column[rows, :]
        for b in range(picks.shape[1] // LANES):
            picks[:, b * LANES : (b + 1) * LANES] = jnp.where(
                own == table_ref[:, b * LANES : (b + 1) * LANES], 1.0, 0.0
            ).astype(BF16)
        dh2 = dot(picks[...], everyone[...])
        low = dh2.astype(BF16)
        dh2_s[rows, :] = low
        du = (dot_nt(low, weights[STARTS[4] : STARTS[5], :]) * slope[rows, :]).astype(BF16)
        du_s[rows, :] = du
        upstream = dot(du, weights[STARTS[3] : STARTS[4], :])
        scaled, spread = standardize(h1[rows, :])
        small[1:2, :] += jnp.sum(upstream * scaled, axis=0, keepdims=True)
        dh1 = dh2 + standardize_back(scaled, spread, gains[1:2, :], upstream)
        dh1_s[rows, :] = dh1
        do = dh1.astype(BF16)
        do_s[rows, :] = do
        dctx[rows, :] = dot_nt(do, weights[STARTS[2] : STARTS[3], :]).astype(BF16)

    for i in range(4):
        part = slice(i * D, (i + 1) * D)
        grads[STARTS[4] + i * D : STARTS[4] + (i + 1) * D, :] = dot_tn(y_in[:, part], dh2_s[...])
        grads[STARTS[3] + i * D : STARTS[3] + (i + 1) * D, :] = dot_tn(du_s[:, part], m_in[...])
    grads[STARTS[2] : STARTS[3], :] = dot_tn(ctx1[...], do_s[...])

    @pl.loop(0, WINS)
    def _(w):
        rows = pl.ds(pl.multiple_of(w * WSZ, 16), WSZ)
        for g in range(GROUPS):
            parts = attend_back(
                probs[w * GROUPS + g],
                r1[rows, group_at(0, g)],
                r1[rows, group_at(1, g)],
                r1[rows, group_at(2, g)],
                dctx[rows, g * LANES : (g + 1) * LANES],
            )
            for i, part in enumerate(parts):
                dr1[rows, group_at(i, g)] = part.astype(BF16)

    @pl.loop(0, TILES)
    def _(t):
        rows = tile_at(t)
        upstream = dot(dr1[rows, :], weights[STARTS[1] : STARTS[2], :])
        scaled, spread = standardize(h0[rows, :].astype(F32))
        small[0:1, :] += jnp.sum(upstream * scaled, axis=0, keepdims=True)
        back = standardize_back(scaled, spread, gains[0:1, :], upstream)
        dh0 = (dh1_s[rows, :] + back).astype(BF16)
        dh0_s[rows, :] = dh0
        small[4:5, :] += ftime * jnp.sum(dh0.astype(F32), axis=0, keepdims=True)

    for i in range(3):
        grads[STARTS[1] + i * D : STARTS[1] + (i + 1) * D, :] = dot_tn(
            dr1[:, i * D : (i + 1) * D], a_in[...]
        )
    grads[STARTS[0] : STARTS[1], :] = dot_tn(joined[...], dh0_s[...])


def adam_update(param, grad, first, second, average, correction, decay_rate, rate):
    first_new = BETA * first + (1.0 - BETA) * grad
    second_new = BETA * second + (1.0 - BETA) * grad * grad
    direction = first_new / correction / (jnp.sqrt(second_new / correction) + EPS_ADAM)
    param_new = param - rate * (direction + decay_rate * param)
    average_new = EMA_RATE * average + (1.0 - EMA_RATE) * param_new
    return (param_new, first_new, second_new, average_new)


def column_table():
    row = np.arange(1024)
    chunk, inner = row // CROWS, row % CROWS
    level, col = inner // 8, inner % 8
    token = level * WSZ + chunk * 16 + col
    return np.where((row < ROWS) & (level < LEV), token, -9).astype(np.int32)


def shape_of(rows, columns, dtype):
    return jax.ShapeDtypeStruct((rows, columns), dtype)


def local(
    noise_draw, single_step, double_step, state_now, target_flag, flow_time, live_count,
    latitude_row, window_order, latitude_weight, level_weight, step_count,
    master_weights, first_moment, second_moment, average_weights,
    gain_rows, gain_first, gain_second, gain_average,
):
    micro = noise_draw.shape[0]
    tokens = noise_draw.shape[1]
    section = lax.axis_index("pipe")
    members = lax.axis_size("dp")
    slot = section // 2
    half = section % 2
    gathered = lax.all_gather(master_weights.astype(BF16), "dp", axis=0, tiled=True)
    weights = natural_order(gathered, members)
    lat_match = latitude_row[:, :, None] == jnp.arange(LATN, dtype=jnp.int32)[None, None, :]
    lat_values = jnp.sum(
        jnp.where(lat_match, latitude_weight.astype(F32)[None, None, :], 0.0), axis=2
    )
    token_weight = (level_weight.astype(F32)[None, :, None] * lat_values[:, None, :]).reshape(
        micro, tokens
    ) * 1e-06
    alive = jnp.arange(tokens, dtype=jnp.int32)[None, :] < live_count
    token_weight = jnp.where(alive, token_weight, 0.0)
    total = lax.psum(jnp.sum(token_weight), "dp")
    inverse_total = 1.0 / (PIN * total)

    def at_slot(values):
        return lax.dynamic_index_in_dim(values, slot, 0, keepdims=False)

    ftime = at_slot(flow_time)[0]
    ints = jnp.stack([slot, half, at_slot(target_flag)[0]])
    floats = jnp.stack([ftime, inverse_total, at_slot(target_flag)[0].astype(F32)])
    order_all = at_slot(window_order)
    order_own = lax.dynamic_slice_in_dim(order_all, half * 864, ROWS, 0)
    order_own = jnp.pad(order_own, (0, 16), constant_values=-1)
    spots = jnp.arange(1024, dtype=jnp.int32)
    order_back = jnp.where((spots < WSZ) & (half > 0), -1, order_own)
    order_pad = jnp.pad(order_all, (0, 48), constant_values=-1)
    table = column_table()
    both = np.full((2048,), -8, np.int32)
    for h in range(2):
        both[h * ROWS : (h + 1) * ROWS] = np.where(table[:ROWS] >= 0, table[:ROWS] + 8 * h, -8)
    weigh = lax.dynamic_index_in_dim(at_slot(token_weight).reshape(LEV, CHUNKS, 2, 8), half, 2, False)
    weigh = jnp.pad(jnp.swapaxes(weigh, 0, 1), ((0, 0), (0, 1), (0, 0))).reshape(1, ROWS)
    weigh = jnp.pad(weigh, ((0, 0), (0, 16)))

    smem = pl.BlockSpec(memory_space=pltpu.SMEM)
    vmem = pl.BlockSpec(memory_space=pltpu.VMEM)
    anym = pl.BlockSpec(memory_space=pl.ANY)
    params = functools.partial(pltpu.CompilerParams, vmem_limit_bytes=VMEM_MAX)

    kept = pl.pallas_call(
        window_forward,
        out_shape=[
            shape_of(ROWS, 2 * PIN, BF16),
            shape_of(ROWS, D, BF16),
            shape_of(ROWS, D, BF16),
            shape_of(ROWS, 3 * D, BF16),
            jax.ShapeDtypeStruct((WINS * GROUPS, PACK * WSZ, WSZ), BF16),
            shape_of(ROWS, D, BF16),
            shape_of(ROWS, D, F32),
            shape_of(ROWS, D, BF16),
            shape_of(ROWS, FF, F32),
            shape_of(ROWS, FF, BF16),
            shape_of(ROWS, D, BF16),
        ],
        in_specs=[smem, smem, anym, anym, anym, anym, vmem, vmem, vmem],
        out_specs=[vmem] * 11,
        scratch_shapes=[
            pltpu.VMEM((1024, LANES), jnp.int32),
            pltpu.VMEM((TILE, 1920), BF16),
            pltpu.VMEM((1920, D), BF16),
            pltpu.VMEM((4, tokens, PIN), BF16),
            pltpu.SemaphoreType.DMA((4,)),
        ],
        compiler_params=params(),
        name="window_forward",
    )(
        ints, floats, noise_draw, single_step, double_step, state_now,
        order_own[None, :], weights[: STARTS[5]], gain_rows,
    )
    h2 = kept[-1]
    grads_late, small_late, everyone = pl.pallas_call(
        column_both,
        out_shape=[shape_of(4 * D + PIN, D, F32), shape_of(8, D, F32), shape_of(2048, D, BF16)],
        in_specs=[smem, anym, anym, anym, vmem, vmem, vmem, vmem, vmem, vmem],
        out_specs=[vmem] * 3,
        scratch_shapes=[
            pltpu.VMEM((1024, LANES), jnp.int32),
            pltpu.VMEM((1024, LANES), F32),
            pltpu.VMEM((TILE, 1920), BF16),
            pltpu.VMEM((1920, D), BF16),
            pltpu.VMEM((ROWS, PIN), F32),
            pltpu.VMEM((3, tokens, PIN), BF16),
            pltpu.VMEM((ROWS, D), BF16),
            pltpu.VMEM((ROWS, D), BF16),
            pltpu.VMEM((ROWS, 3 * D), BF16),
            pltpu.VMEM((CHUNKS * GROUPS, PACK * CROWS, CROWS), F32),
            pltpu.VMEM((ROWS, D), BF16),
            pltpu.VMEM((ROWS, D), BF16),
            pltpu.VMEM((ROWS, D), BF16),
            pltpu.VMEM((ROWS, D), BF16),
            pltpu.VMEM((ROWS, PIN), BF16),
            pltpu.VMEM((ROWS, 3 * D), BF16),
            pltpu.SemaphoreType.DMA((3,)),
            pltpu.SemaphoreType.DMA((2,)),
            pltpu.SemaphoreType.DMA((2,)),
        ],
        compiler_params=params(collective_id=0, has_side_effects=True),
        name="column_both",
    )(
        floats, noise_draw, single_step, double_step, h2, order_pad[None, :],
        jnp.asarray(table)[None, :], weigh, weights[STARTS[5] :], gain_rows,
    )
    grads_early, small_early = pl.pallas_call(
        window_backward,
        out_shape=[shape_of(STARTS[5], D, F32), shape_of(8, D, F32)],
        in_specs=[smem] + [vmem] * 15,
        out_specs=[vmem] * 2,
        scratch_shapes=[
            pltpu.VMEM((1024, LANES), jnp.int32),
            pltpu.VMEM((TILE, 2048), BF16),
            pltpu.VMEM((ROWS, D), BF16),
            pltpu.VMEM((ROWS, FF), BF16),
            pltpu.VMEM((ROWS, D), F32),
            pltpu.VMEM((ROWS, D), BF16),
            pltpu.VMEM((ROWS, D), BF16),
            pltpu.VMEM((ROWS, 3 * D), BF16),
            pltpu.VMEM((ROWS, D), BF16),
        ],
        compiler_params=params(),
        name="window_backward",
    )(
        floats, everyone, order_back[None, :], jnp.asarray(both)[None, :],
        weights[: STARTS[5]], gain_rows, *kept[:-1],
    )
    grads = stored_order(jnp.concatenate([grads_early, grads_late], axis=0), members)
    shard = lax.psum(lax.psum_scatter(grads, "dp", scatter_dimension=0, tiled=True), "pipe")
    gains_part = jnp.stack(
        [small_early[0], small_early[1], small_late[0], small_late[1], small_early[4]]
    )
    gain_total, loss_total = lax.psum((gains_part, jnp.sum(small_late[2])), ("dp", "pipe"))
    square_total = lax.psum(jnp.sum(shard * shard), "dp")
    grad_norm = jnp.sqrt(square_total + jnp.sum(gain_total * gain_total))
    factor = jnp.minimum(1.0, CLIP_MAX / (grad_norm + 1e-06))
    correction = 1.0 - jnp.power(0.5, step_count[0].astype(F32))
    new_weights, new_first, new_second, new_average = adam_update(
        master_weights, factor * shard, first_moment, second_moment, average_weights,
        correction, DECAY_WEIGHT, RATE,
    )
    new_gains, new_gain_first, new_gain_second, new_gain_average = adam_update(
        gain_rows, factor * gain_total, gain_first, gain_second, gain_average,
        correction, 0.0, GAIN_RATE,
    )
    return (
        loss_total, grad_norm, new_weights, new_first, new_second, new_average,
        new_weights.astype(BF16), new_gains, new_gain_first, new_gain_second, new_gain_average,
    )


def solution(mesh):
    over = P("dp", None)
    token = P(None, "dp", None)
    pair = P(None, "dp")
    in_specs = (token,) * 4 + (pair,) * 5 + (P(),) * 3 + (over,) * 4 + (P(),) * 4
    out_specs = (P(), P()) + (over,) * 5 + (P(),) * 4
    return jax.shard_map(local, mesh=mesh, in_specs=in_specs, out_specs=out_specs, check_vma=False)
```

time: 2030 us -> 488 us (0.24)
  waiting for transfers between devices: 1190 us -> 224 us
  starting transfers between devices: 460 us -> 0.12 us
  loops' own time: 136 us -> 0 us
  Pallas kernels: 0 us -> 110 us
  local copies, waits for them, and re-layouts: 72.8 us -> 29.5 us
  other arithmetic: 55.1 us -> 19.9 us
    ppermute x10 -> x0, waiting for transfers between devices: 974 us -> none  [passed_along(): return lax.ppermute(value, axis, pairs)]
    ppermute x10 -> x0, starting transfers between devices: 460 us -> none  [passed_along(): return lax.ppermute(value, axis, pairs)]
    reduce_scatter x0 -> x1, waiting for transfers between devices: none -> 170 us  [local(): lax.psum_scatter(grads, 'dp', scatter_dimension=0, tiled=True)]
    psum x1, waiting for transfers between devices: 155 us -> 0.01 us  [local(): lax.psum(lax.psum_scatter(grads, 'dp', scatter_dimension=0, tiled=True),...]
    another operation x12 -> x0, loops' own time: 136 us -> none  [the longest x5 113 us: backward_tick(): lax.switch(branch_index, [encode_back, swin_back, column_back, decode_bac...]
    pallas_call x0 -> x3, Pallas kernels: none -> 110 us  [the longest x1 41.1 us: local(): pl.pallas_call(window_backward, out_shape=[shape_of(STARTS[5], D, F32), s...]
    psum x1 -> x2, blocking collectives: 55.7 us -> 61.7 us  [the longest x1 40 us: local(): lax.psum((gains_part, jnp.sum(small_late[2])), ('dp', 'pipe'))]
  transfers between devices with their start and end apart: 12 -> 3, of which waited for: 7 -> 2; matrix products, arithmetic and copies ran while one was open for 1% -> 3% of each run, Pallas kernels for 0% -> 0%
where the time goes in v1:
time: 488 us; the launch traced here: 487 us
  waiting for transfers between devices  224 us (46%)
  Pallas kernels  110 us (23%)
  blocking collectives  85.9 us (18%)
  local copies, waits for them, and re-layouts  29.5 us (6%)
  other arithmetic  19.9 us (4%)
  between operations  18.1 us (4%)
    reduce_scatter x1, waiting for transfers between devices, local(): lax.psum_scatter(grads, 'dp', scatter_dimension=0, tiled=True)  170 us
    all_gather x1, waiting for transfers between devices, local(): lax.all_gather(master_weights.astype(BF16), 'dp', axis=0, tiled=True)  53.6 us
    pallas_call x1, Pallas kernels, local(): pl.pallas_call(window_backward, out_shape=[shape_of(STARTS[5], D, F32), s...  41.1 us
    psum x1, blocking collectives, local(): lax.psum((gains_part, jnp.sum(small_late[2])), ('dp', 'pipe'))  40 us
    pallas_call x1, Pallas kernels, local(): pl.pallas_call(column_both, out_shape=[shape_of(4 * D + PIN, D, F32), sha...  37.1 us
    pallas_call x1, Pallas kernels, local(): pl.pallas_call(window_forward, out_shape=[shape_of(ROWS, 2 * PIN, BF16),...  31.6 us
    psum x1, blocking collectives, local(): total = lax.psum(jnp.sum(token_weight), 'dp')  24.2 us
    psum x1, blocking collectives, local(): square_total = lax.psum(jnp.sum(shard * shard), 'dp')  21.7 us
  transfers between devices with their start and end apart: 3, of which 2 were waited for; matrix products, arithmetic and copies ran while one was open for 3% of the time, Pallas kernels for 0%

profile of v1, /device:TPU:0, one launch (start us, length us, event | category | flops | bytes accessed | tf_op | source)
XLA Modules:
  0.0 487.3 jit_solution(1131614442206551805)
XLA Ops:
  7.3 2.2 convert_element_type.27
  10.5 24.2 %psum.35 = f32[]{:T(128)} all-reduce(f32[]{:T(128)} %select_reduce_fusion), channel_id=1, replica_groups=mesh['dp'=8,'pipe'=4] {'dp'}, use_global_device_ids=true, to_apply=%region_2.3 | all-reduce | flops 1 | bytes 8 | tf_op jit(solution)/shard_map/psum | solution.py:498
  39.8 1.3 pad_add_fusion.ints
  41.1 1.9 pad_maximum_fusion.2.floats
  43.6 53.6 %all-gather.2.cloned.1.call-done = bf16[6528,384]{1,0:T(8,128)(2,1)} async-done(((bf16[816,384]{1,0:T(8,128)(2,1)}), bf16[6528,384]{1,0:T(8,128)(2,1)}) %all-gather.2.cloned.1.call-update) | async-done | bytes 5013520 | tf_op jit(solution)/shard_map/all_gather | solution.py:487
  97.2 1.6 fusion.11
  98.8 1.0 slice.89
  99.7 1.1 fusion.12
  100.9 1.9 fusion.13
  102.7 0.9 slice.96
  104.4 1.3 pad_maximum_fusion.weights
  105.7 0.9 copy-done.2
  106.7 31.6 %window_forward.1 = (bf16[1008,256]{1,0:T(8,128)(2,1)}, bf16[1008,384]{1,0:T(8,128)(2,1)}, bf16[1008,384]{1,0:T(8,128)(2,1)}, bf16[1008,1152]{1,0:T(8,128)(2,1)}...) custom-call(s32[3]{0:T(128)} %pad_add_fusion.ints, ...), custom_call_target="tpu_custom_call" | custom-call | tf_op jit(solution)/shard_map/window_forward/pallas_call | solution.py:526
  138.2 37.1 %column_both.1 = (f32[1664,384]{1,0:T(8,128)}, f32[8,384]{1,0:T(8,128)}, bf16[2048,384]{1,0:T(8,128)(2,1)}) custom-call(f32[3]{0:T(128)} %pad_maximum_fusion.2.floats, bf16[2,1872,128]{2,1,0:T(8,128)(2,1)} %noise_any.3, bf16[2,1872,128]{2,1,0:T(8,128)(2,1)} %single_any.3, bf16[2,1872,128]{2,1,0:T(8,128)(2,1)} %double_any.3, ...), custom_call_target="tpu_custom_call" | custom-call | tf_op jit(solution)/shard_map/column_both/pallas_call | solution.py:557
  175.3 41.1 %window_backward.1 = (f32[4864,384]{1,0:T(8,128)}, f32[8,384]{1,0:T(8,128)}) custom-call(f32[3]{0:T(128)} %pad_maximum_fusion.2.floats, bf16[2048,384]{1,0:T(8,128)(2,1)} %get-tuple-element.29.everyone, s32[1,1024]{1,0:T(1,128)} %bitcast.57, s32[1,2048]{1,0:T(1,128)} %constant.124.table_ref, bf16[4864,384]{1,0:T(8,128)(2,1)} %copy-done.2, f32[5,384]{1,0:T(8,128)} %gains.5, ...), custom_call_target="tpu_custom_call" | custom-call | tf_op jit(solution)/shard_map/window_backward/pallas_call | solution.py:589
  216.4 1.0 slice.78
  217.5 1.6 slice.79
  219.0 1.1 slice.80
  220.2 2.8 fusion.10
  224.3 1.3 constant_dynamic-update-slice_fusion.11
  225.6 0.8 constant_dynamic-update-slice_fusion.10
  226.4 1.6 constant_dynamic-update-slice_fusion.9
  228.1 1.6 constant_dynamic-update-slice_fusion.8
  229.6 1.3 constant_dynamic-update-slice_fusion.7
  230.9 0.9 constant_dynamic-update-slice_fusion.6
  232.6 170.5 %reduce-scatter.2.cloned.1.call-done = f32[816,384]{1,0:T(8,128)} async-done(((f32[6528,384]{1,0:T(8,128)}), f32[816,384]{1,0:T(8,128)}) %reduce-scatter.2.cloned.1.call-update) | async-done | bytes 1253392 | tf_op jit(solution)/shard_map/reduce_scatter | solution.py:612
  406.0 1.3 slice_reduce_fusion
  407.3 40.0 %all-reduce.4 = (f32[]{:T(128)}, f32[5,384]{1,0:T(8,128)S(1)}) all-reduce(f32[]{:T(128)} %slice_reduce_fusion, f32[5,384]{1,0:T(8,128)S(1)} %pad_maximum_fusion.1), channel_id=1, replica_groups=mesh['dp'=8,'pipe'=4] {'dp','pipe'}, use_global_device_ids=true, to_apply=%region_4.5 | all-reduce | flops 1921 | bytes 15368 | tf_op jit(solution)/shard_map/psum | solution.py:616
  447.3 2.3 multiply_reduce_fusion
  450.2 21.7 %psum.38 = f32[]{:T(128)} all-reduce(f32[]{:T(128)} %multiply_reduce_fusion), channel_id=1, replica_groups=mesh['dp'=8,'pipe'=4] {'dp'}, use_global_device_ids=true, to_apply=%region_8.9 | all-reduce | flops 1 | bytes 8 | tf_op jit(solution)/shard_map/psum | solution.py:617
  473.3 4.2 fusion.8
  477.6 1.4 multiply_add_fusion.1
  (82 shorter events, 12.2 us)
Async XLA Ops:
  7.2 28.1 %copy-start = (f32[2,1]{0,1:T(1,128)S(1)}, f32[2,1]{0,1:T(1,128)}, u32[]{:S(2)}) copy-start(f32[2,1]{0,1:T(1,128)} %param.27) | copy-start | bytes 28
  7.2 2.4 copy-start.16
  7.2 2.4 copy-start.17
  7.2 2.4 copy-start.13
  7.2 2.6 copy-start.14
  7.2 30.6 %copy-start.12 = (s32[2,1872]{1,0:T(2,128)S(1)}, s32[2,1872]{1,0:T(2,128)}, u32[]{:S(2)}) copy-start(s32[2,1872]{1,0:T(2,128)} %param.30) | copy-start | bytes 44932
  7.2 32.0 %copy-start.15 = (s32[2,1]{0,1:T(1,128)S(1)}, s32[2,1]{0,1:T(1,128)}, u32[]{:S(2)}) copy-start(s32[2,1]{0,1:T(1,128)} %param.26) | copy-start | bytes 28
  7.3 89.9 %all-gather.2.cloned.1.call-start = ((), (), s32[]{:S(2)}) async-start(), calls=%async_computation.1 | async-start | bytes 5640192 | tf_op jit(solution)/shard_map/all_gather | solution.py:487
  9.5 393.6 %reduce-scatter.2.cloned.1.call-start = ((), (), s32[]{:S(2)}) async-start(), calls=%async_computation.2 | async-start | bytes 11280384 | tf_op jit(solution)/shard_map/reduce_scatter | solution.py:612
  104.4 2.2 copy-start.2
  220.2 3.1 copy-start.6
  232.5 240.8 %copy-start.3 = (f32[816,384]{1,0:T(8,128)S(1)}, f32[816,384]{1,0:T(8,128)}, u32[]{:S(2)}) copy-start(f32[816,384]{1,0:T(8,128)} %param.34) | copy-start | bytes 3760132
  232.6 214.8 %all-reduce.7.cloned.1.call-start = ((), (), s32[]{:S(2)}) async-start(), calls=%async_computation.3 | async-start | bytes 2506752 | tf_op jit(solution)/shard_map/psum | solution.py:612
  447.3 26.0 %copy-start.4 = (f32[816,384]{1,0:T(8,128)S(1)}, f32[816,384]{1,0:T(8,128)}, u32[]{:S(2)}) copy-start(f32[816,384]{1,0:T(8,128)} %all-reduce.7.cloned.1.call-done) | copy-start | bytes 3760132
  473.3 4.2 copy-start.7
  477.5 1.5 copy-start.5
  477.5 2.1 copy-start.1
  477.5 1.4 copy-start.8
  477.6 1.4 copy-start.9
  477.6 1.4 copy-start.10
  477.6 1.4 copy-start.11
Sparse Core Ops, SparseCore 0:
  10.8 86.2 all-gather.1
  232.7 170.3 reduce-scatter.1
  405.5 38.0 all-reduce.6

commit v2 on v1

v2 whole, which is shorter than its diff:
```python
import functools
from types import SimpleNamespace

import jax
import jax.numpy as jnp
import numpy as np
from jax import lax
from jax.experimental import pallas as pl
from jax.experimental.pallas import tpu as pltpu
from jax.sharding import PartitionSpec as P

D = 384
HEADS = 12
HD = 32
FF = 1536
PIN = 128
LEV = 13
WSZ = 144
LATN = 60

EPS_NORM = 1e-05
CLIP_MAX = 0.01
RATE = 0.03
GAIN_RATE = 0.3
BETA = 0.5
EPS_ADAM = 1e-08
DECAY_WEIGHT = 0.05
EMA_RATE = 0.8

F32 = jnp.float32
BF16 = jnp.bfloat16
MESH = pl.DeviceIdType.MESH

SOFT = HD ** (-0.5) * 1.4426950408889634
GROUPS = 3
PACK = 4
LANES = 128

ROWS = 1008
TILE = 336
TILES = 3
WINS = 7
CHUNKS = 9
CROWS = 112
VMEM_MAX = 63 * 2**20


def block_starts():
    widths = [2 * PIN, 3 * D, D, FF, FF, 3 * D, D, PIN]
    starts = [0]
    for width in widths:
        starts.append(starts[-1] + width)
    return starts


STARTS = block_starts()


def natural_order(stored, pieces_count):
    view = stored.reshape(pieces_count, stored.shape[0] // pieces_count, stored.shape[1])
    pieces = []
    for number in range(8):
        pieces.append(
            view[:, STARTS[number] // pieces_count : STARTS[number + 1] // pieces_count].reshape(
                -1, stored.shape[1]
            )
        )
    return jnp.concatenate(pieces, axis=0)


def stored_order(natural, pieces_count):
    pieces = []
    for number in range(8):
        pieces.append(
            natural[STARTS[number] : STARTS[number + 1]].reshape(pieces_count, -1, natural.shape[1])
        )
    return jnp.concatenate(pieces, axis=1).reshape(-1, natural.shape[1])


def dot(left, right):
    return jnp.dot(left, right, preferred_element_type=F32)


def dot_nt(left, right):
    return lax.dot_general(left, right, (((1,), (1,)), ((), ())), preferred_element_type=F32)


def dot_tn(left, right):
    return lax.dot_general(left, right, (((0,), (0,)), ((), ())), preferred_element_type=F32)


def standardize(values):
    center = values - jnp.mean(values, axis=-1, keepdims=True)
    spread = lax.rsqrt(jnp.mean(center * center, axis=-1, keepdims=True) + EPS_NORM)
    return center * spread, spread


def standardize_back(scaled, spread, gain, upstream):
    inner = upstream * gain
    return spread * (
        inner
        - jnp.mean(inner, axis=-1, keepdims=True)
        - scaled * jnp.mean(inner * scaled, axis=-1, keepdims=True)
    )


def head_masks(dtype):
    lane = lax.broadcasted_iota(jnp.int32, (1, LANES), 1) // HD
    return [jnp.where(lane == h, 1.0, 0.0).astype(dtype) for h in range(PACK)]


def spread_heads(block):
    return jnp.concatenate([block * mask for mask in head_masks(block.dtype)], axis=0)


def gather_heads(stacked, n):
    masks = head_masks(F32)
    total = stacked[0:n] * masks[0]
    for h in range(1, PACK):
        total = total + stacked[h * n : (h + 1) * n] * masks[h]
    return total


def attend(query, keys, values, keep):
    n = query.shape[0]
    scores = dot_nt(spread_heads(keys), query)
    if keep is not None:
        scores = jnp.where(keep, scores, -1e30)
    blocks = scores.reshape(PACK, n, n)
    top = jnp.max(blocks, axis=1, keepdims=True)
    expo = jnp.exp2((blocks - top) * SOFT)
    probs = expo * (1.0 / jnp.sum(expo, axis=1, keepdims=True))
    probs = probs.reshape(PACK * n, n)
    context = dot_tn(probs.astype(BF16), spread_heads(values))
    return probs, context


def attend_back(probs, query, keys, values, upstream):
    n = query.shape[0]
    probs_low = probs.astype(BF16)
    wide = probs.astype(F32).reshape(PACK, n, n)
    grad_values = gather_heads(dot(probs_low, upstream), n)
    grad_probs = dot_nt(spread_heads(values), upstream).reshape(PACK, n, n)
    delta = jnp.sum(wide * grad_probs, axis=1, keepdims=True)
    grad_scores = (wide * (grad_probs - delta)).astype(BF16).reshape(PACK * n, n)
    factor = HD ** (-0.5)
    grad_query = dot_tn(grad_scores, spread_heads(keys)) * factor
    grad_keys = gather_heads(dot(grad_scores, query), n) * factor
    return grad_query, grad_keys, grad_values


def column_of(row):
    wide = jnp.broadcast_to(row.astype(F32), (LANES, row.shape[1]))
    return jnp.transpose(wide)


def tile_at(t):
    return pl.ds(pl.multiple_of(t * TILE, 16), TILE)


def group_at(which, g):
    start = which * D + g * LANES
    return slice(start, start + LANES)


WIDTHS = (2 * PIN, 3 * D, D, FF, FF, 3 * D, D, PIN)
NAMES = ("E", "A1", "O1", "U", "V", "A2", "O2", "Q")
PACKED = dict(E=0, Q=32, A1=64, O1=208, U=256, V=448, A2=640, O2=784)
PACKED_ROWS = 832
SHARDS = 8
GATHERS = ((0, 64, False), (64, 192, False), (256, 192, True), (448, 192, True), (640, 192, True))
SUMS = dict(L=(640, 192), V=(448, 192), U=(256, 192), N=(64, 192), O=(0, 64))


class Plan:
    def __init__(self, direct):
        self.direct = direct
        self.shape = (4, 2) if direct else (1, 1)
        self.count = self.shape[0] * self.shape[1]
        self.rows = PACKED_ROWS if direct else STARTS[8]
        self.offsets = {}
        for name, start, width in zip(NAMES, STARTS, WIDTHS):
            self.offsets[name] = (
                PACKED[name] if direct else start,
                width // self.count,
            )

    def load(self, ref, name):
        start, size = self.offsets[name]
        return ref[:, :, start : start + size, :].reshape(self.count * size, D)

    def store(self, ref, name, value):
        start, size = self.offsets[name]
        ref[:, :, start : start + size, :] = value.astype(ref.dtype).reshape(*self.shape, size, D)


    def store_part(self, ref, name, i, value):
        start, size = self.offsets[name]
        if self.direct:
            ref[i, :, start : start + size, :] = value.astype(ref.dtype).reshape(2, size, D)
        else:
            ref[0, 0, start + i * D : start + (i + 1) * D, :] = value.astype(ref.dtype)


class Mail:
    def __init__(self, send_sems, recv_sems):
        self.sems = (send_sems, recv_sems)
        self.table = {}

    def add(self, key, source, target, device):
        index = len(self.table)

        def build():
            return pltpu.make_async_remote_copy(
                src_ref=source(),
                dst_ref=target(),
                send_sem=self.sems[0].at[index],
                recv_sem=self.sems[1].at[index],
                device_id=device,
                device_id_type=MESH,
            )

        self.table[key] = build

    def start(self, *keys):
        for key in keys:
            self.table[key]().start()

    def wait(self, *keys):
        for key in keys:
            self.table[key]().wait_recv()

    def close(self):
        for build in self.table.values():
            build().wait_send()


MESSAGES = 120


def aligned(start, size):
    return pl.ds(pl.multiple_of(start, 16), size)


def step_kernel(plan, names, *refs):
    r = SimpleNamespace(**dict(zip(names, refs)))
    dp = lax.axis_index("dp")
    pipe = lax.axis_index("pipe")
    slot, half = pipe // 2, lax.rem(pipe, 2)
    y, c = slot, half
    z, x = dp // 2, lax.rem(dp, 2)
    mail = Mail(r.send_sems, r.recv_sems)
    wts, grads, gains = r.wts, r.grads, r.gains

    def at(z_to, x_to, y_to, c_to):
        return {"dp": z_to * 2 + x_to, "pipe": y_to * 2 + c_to}

    partner = {"pipe": pipe + 1 - 2 * half}
    rings = [lax.rem(z + k, 4) for k in (1, 2, 3)]
    plane = [(1 - x, y), (x, 1 - y), (1 - x, 1 - y)]
    mates = [(1 - y, c), (y, 1 - c), (1 - y, 1 - c)]

    barrier = pltpu.get_barrier_semaphore()
    if plan.direct:
        peers = [at(to, x, y, c) for to in rings]
        peers += [at(z, tx, ty, c) for tx, ty in plane]
        peers += [at(z, x, y, 1 - c), at(z, x, 1 - y, 1 - c)]
        peers += [at(to, 1 - x, y, c) for to in rings]
    else:
        peers = [partner]
    for peer in peers:
        pl.semaphore_signal(barrier, inc=1, device_id=peer, device_id_type=MESH)

    loads = {}
    local_sems = r.local_sems

    def load(key, source, target):
        loads[key] = pltpu.make_async_copy(source, target, local_sems.at[len(loads)])
        loads[key].start()

    if plan.direct:
        at_row = 0
        for name, width in zip(NAMES, WIDTHS):
            size = width // SHARDS
            load(
                "w" + name,
                r.master.at[pl.ds(at_row, size), :],
                r.h1.at[pl.ds(PACKED[name], size), :],
            )
            at_row += size
    else:
        load("w", r.weights_in, wts.at[0, 0])
    source, raw = r.source, r.raw
    tokens = raw.shape[0]
    for i, (name, ref) in enumerate((("noise", r.noise), ("single", r.single), ("state", r.state))):
        load(name, ref.at[slot], source.at[pl.ds(0, tokens), pl.ds(i * PIN, PIN)])
    load("double", r.double.at[slot], raw)

    allh, everyone = r.allh, r.everyone
    base = pl.multiple_of(half * ROWS, 16)
    mail.add(
        "h2",
        lambda: allh.at[aligned(half * ROWS, 864), :],
        lambda: allh.at[aligned(half * ROWS, 864), :],
        partner,
    )
    mail.add(
        "dh2",
        lambda: everyone.at[pl.ds(base, ROWS), :],
        lambda: everyone.at[pl.ds(base, ROWS), :],
        partner,
    )
    if plan.direct:

        def same(key, view, device):
            mail.add(key, view, view, device)

        own = []
        for g, (start, rows, quartered) in enumerate(GATHERS):
            size = rows // 4 if quartered else rows // 2
            mine = aligned(start + (2 * y + c if quartered else c) * size, size)
            other = aligned(start + (2 * (1 - y) + c) * size, size)
            own.append(mine)
            for k, to in enumerate(rings):
                same(f"gz{g}{k}", lambda mine=mine: wts.at[z, x, mine, :], at(to, x, y, c))
            same(f"gx{g}", lambda mine=mine: wts.at[:, x, mine, :], at(z, 1 - x, y, c))
            if quartered:
                same(f"gy{g}", lambda mine=mine: wts.at[:, :, mine, :], at(z, x, 1 - y, c))
                same(f"gc{g}", lambda mine=mine: wts.at[:, :, mine, :], at(z, x, y, 1 - c))
                same(f"gd{g}", lambda other=other: wts.at[:, :, other, :], at(z, x, y, 1 - c))
            else:
                same(f"gc{g}", lambda mine=mine: wts.at[:, x, mine, :], at(z, x, y, 1 - c))
                same(f"gd{g}", lambda mine=mine: wts.at[:, 1 - x, mine, :], at(z, x, y, 1 - c))
        tot, tot_z, tot_x = r.tot, r.tot_z, r.tot_x
        for k, to in enumerate(rings):
            mail.add(f"tz{k}", lambda: tot_z.at[z], lambda: tot_z.at[z], at(to, x, y, c))
        mail.add("tx", lambda: tot, lambda: tot_x, at(z, 1 - x, y, c))
        pair_in, plane_in, ring_out, ring_in, final = (
            r.pair_in, r.plane_in, r.ring_out, r.ring_in, r.final,
        )
        for key, (start, rows) in SUMS.items():
            h, q = rows // 2, rows // 4
            away = aligned(start + (1 - c) * h, h)
            mail.add(
                key + "c",
                lambda away=away: grads.at[:, :, away, :],
                lambda start=start, h=h: pair_in.at[:, :, pl.ds(start // 2, h), :],
                at(z, x, y, 1 - c),
            )
            for k, (tx, ty) in enumerate(plane):
                piece = aligned(start + c * h + ty * q, q)
                mail.add(
                    f"{key}p{k}",
                    lambda tx=tx, piece=piece: grads.at[:, tx, piece, :],
                    lambda k=k, start=start, q=q: plane_in.at[k, :, pl.ds(start // 4, q), :],
                    at(z, tx, ty, c),
                )
            for k, to in enumerate(rings):
                mail.add(
                    f"{key}z{k}",
                    lambda to=to, start=start, q=q: ring_out.at[to, pl.ds(start // 4, q), :],
                    lambda start=start, q=q: ring_in.at[z, pl.ds(start // 4, q), :],
                    at(to, x, y, c),
                )
            done = aligned(start + c * h + y * q, q)
            for k, (ty, tc) in enumerate(mates):
                same(f"{key}g{k}", lambda done=done: final.at[done, :], at(z, x, ty, tc))
        small, small_c, small_p, small_z = r.small, r.small_c, r.small_p, r.small_z
        mail.add("sc", lambda: small.at[0], lambda: small_c, at(z, x, y, 1 - c))
        for k, (tx, ty) in enumerate(plane):
            mail.add(f"sp{k}", lambda: small.at[1], lambda k=k: small_p.at[k], at(z, tx, ty, c))
        for k, to in enumerate(rings):
            mail.add(f"sz{k}", lambda: small_z.at[z], lambda: small_z.at[z], at(to, x, y, c))
        square = r.square
        for k in range(1, SHARDS):
            to = lax.rem(dp + k, SHARDS)
            mail.add(
                f"n{k}",
                lambda: square.at[dp],
                lambda: square.at[dp],
                {"dp": to, "pipe": pipe},
            )

    def sum_pair(key):
        start, rows = SUMS[key]
        h = rows // 2
        mail.wait(key + "c")
        keep = aligned(start + c * h, h)
        for i in range(4):
            grads[i, :, keep, :] = (
                grads[i, :, keep, :].astype(F32)
                + pair_in[i, :, start // 2 : start // 2 + h, :].astype(F32)
            ).astype(BF16)
        mail.start(*(f"{key}p{k}" for k in range(3)))

    def sum_plane(key):
        start, rows = SUMS[key]
        h, q = rows // 2, rows // 4
        mail.wait(*(f"{key}p{k}" for k in range(3)))
        keep = aligned(start + c * h + y * q, q)
        spot = slice(start // 4, start // 4 + q)
        total = grads[:, x, keep, :].astype(F32)
        for k in range(3):
            total = total + plane_in[k, :, spot, :].astype(F32)
        ring_out[:, spot, :] = total.astype(BF16)
        ring_in[z, spot, :] = ring_out[z, spot, :]
        mail.start(*(f"{key}z{k}" for k in range(3)))

    def sum_ring(key):
        start, rows = SUMS[key]
        h, q = rows // 2, rows // 4
        mail.wait(*(f"{key}z{k}" for k in range(3)))
        spot = slice(start // 4, start // 4 + q)
        total = ring_in[0, spot, :].astype(F32)
        for k in range(1, 4):
            total = total + ring_in[k, spot, :].astype(F32)
        final[aligned(start + c * h + y * q, q), :] = total.astype(BF16)
        mail.start(*(f"{key}g{k}" for k in range(3)))

    def direct(function, *values):
        if plan.direct:
            function(*values)

    lat = jnp.zeros(r.lat_row.shape, F32)
    columns = lat.shape[1]
    for j in range(LATN):
        lat = jnp.where(r.lat_row[...] == j, r.lat_weight[j].astype(F32), lat)
    live = jnp.concatenate(
        [jnp.full((1, columns), r.live[0, i], jnp.int32) for i in range(lat.shape[0])], axis=0
    )
    if plan.direct:
        summed = jnp.zeros(lat.shape, F32)
        for lev in range(LEV):
            token = lax.broadcasted_iota(jnp.int32, lat.shape, 1) + lev * columns
            weigh = r.lev_weight[lev].astype(F32) * lat * 1e-06
            summed = summed + jnp.where(token < live, weigh, 0.0)
        summed = jnp.sum(jnp.sum(summed, axis=1, keepdims=True), axis=0, keepdims=True)
        tot_z[z] = jnp.broadcast_to(summed, (8, LANES))
    pl.semaphore_wait(barrier, len(peers))
    if plan.direct:
        mail.start("tz0", "tz1", "tz2")
        for name in NAMES:
            loads["w" + name].wait()
        r.h1[48:64, :] = jnp.zeros((16, D), F32)
        for g, mine in enumerate(own):
            wts[z, x, mine, :] = r.h1[mine, :].astype(BF16)
            mail.start(*(f"gz{g}{k}" for k in range(3)))

    order_row, order_col = r.order_row, r.order_col
    order_row[...] = jnp.full(order_row.shape, -1, jnp.int32)
    order_row[:, :tokens] = jnp.where(slot > 0, r.order[1:2, :], r.order[0:1, :])
    order_col[...] = column_of(order_row[...]).astype(jnp.int32)
    table = column_of(r.table[...]).astype(jnp.int32)
    column = r.column
    column[...] = jnp.where(table >= 0, table + 8 * half, -9)
    lat_own = jnp.where(slot > 0, lat[1:2, :], lat[0:1, :])
    lat_col = r.lat_col
    lat_col[...] = column_of(
        jnp.concatenate([lat_own, jnp.zeros((1, lat_col.shape[0] - columns), F32)], axis=1)
    )
    live_own = jnp.full((1, LANES), r.live[0, slot], jnp.int32)
    ftime = r.ftime[0, slot]
    pick_double = r.flag[0, slot].astype(F32)
    token_w, velocity = r.token_w, r.velocity
    for name in ("noise", "single", "double", "state"):
        loads[name].wait()
    picks, joined = r.picks, r.joined
    second = jnp.full((1, PIN), pick_double, F32).astype(BF16)
    first = jnp.full((1, PIN), 1.0 - pick_double, F32).astype(BF16)
    source[tokens:, :] = jnp.zeros((source.shape[0] - tokens, D), BF16)
    source[:tokens, PIN : 2 * PIN] = source[:tokens, PIN : 2 * PIN] * first + raw[...] * second
    lane = lax.broadcasted_iota(jnp.int32, (1, LANES), 1)

    @pl.loop(0, TILES)
    def _(t):
        rows = tile_at(t)
        spots = order_col[aligned(half * 864 + t * TILE, TILE), :]
        for b in range(1920 // LANES):
            picks[:, b * LANES : (b + 1) * LANES] = jnp.where(
                spots == lane + b * LANES, 1.0, 0.0
            ).astype(BF16)
        drawn = dot(picks[:, :1920], source[...])
        noisy = (1.0 - ftime) * drawn[:, 0:PIN] + ftime * drawn[:, PIN : 2 * PIN]
        joined[rows, 0:PIN] = noisy.astype(BF16)
        joined[rows, PIN:] = drawn[:, 2 * PIN :].astype(BF16)

    if plan.direct:
        mail.wait("tz0", "tz1", "tz2")
        tot[...] = ((tot_z[0] + tot_z[1]) + tot_z[2]) + tot_z[3]
        mail.start("tx")
        for g in (0, 1):
            mail.wait(*(f"gz{g}{k}" for k in range(3)))
            mail.start(f"gx{g}", f"gc{g}")

    @pl.loop(0, CHUNKS)
    def _(k):
        for lev in range(LEV):
            spot = pl.ds(pl.multiple_of(lev * WSZ + k * 16, 16), 16)
            rows = pl.ds(pl.multiple_of(k * CROWS + lev * 8, 8), 8)
            speed = source[spot, PIN : 2 * PIN].astype(F32) - source[spot, 0:PIN].astype(F32)
            velocity[rows, :] = jnp.where(half > 0, speed[8:16], speed[0:8])
            weigh = (
                r.lev_weight[lev].astype(F32)
                * lat_col[pl.ds(pl.multiple_of(k * 16 + half * 8, 8), 8), :]
                * 1e-06
            )
            token_w[rows, :] = jnp.where(column[rows, :] < live_own, weigh, 0.0)
        rows = pl.ds(pl.multiple_of(k * CROWS + LEV * 8, 8), 8)
        velocity[rows, :] = jnp.zeros((8, PIN), F32)
        token_w[rows, :] = jnp.zeros((8, LANES), F32)

    if plan.direct:
        for g in (2, 3, 4):
            mail.wait(*(f"gz{g}{k}" for k in range(3)))
            mail.start(f"gx{g}")
        mail.wait("tx")
        r.scale[...] = 1.0 / (PIN * (tot[...] + r.tot_x[...]))
        for g in (0, 1):
            mail.wait(f"gx{g}")
            mail.start(f"gd{g}")
        mail.wait("gc0", "gd0", "gc1", "gd1")
    else:
        r.scale[...] = jnp.broadcast_to(r.scale_in[0:1, :], (8, LANES))
        loads["w"].wait()

    h0, a_s, r1, ctx1 = r.h0, r.a, r.r1, r.ctx1
    probs1, h1, m_s, slope, y_s = r.probs1, r.h1, r.m, r.slope, r.y

    @pl.loop(0, TILES)
    def _(t):
        rows = tile_at(t)
        low = (dot(joined[rows, :], plan.load(wts, "E")) + ftime * gains[4:5, :]).astype(BF16)
        h0[rows, :] = low
        scaled, _ = standardize(low.astype(F32))
        normed = (scaled * gains[0:1, :]).astype(BF16)
        a_s[rows, :] = normed
        r1[rows, :] = dot_nt(normed, plan.load(wts, "A1")).astype(BF16)

    def gather_x(g):
        mail.wait(f"gx{g}")
        mail.start(f"gy{g}", f"gc{g}")

    def gather_y(g):
        mail.wait(f"gy{g}")
        mail.start(f"gd{g}")

    def pump(index, steps):
        if plan.direct:
            for k, step in enumerate(steps):
                if step is not None:
                    pl.when(index == k)(step)

    @pl.loop(0, WINS)
    def _(w):
        rows = pl.ds(pl.multiple_of(w * WSZ, 16), WSZ)
        for g in range(GROUPS):
            p, context = attend(
                r1[rows, group_at(0, g)], r1[rows, group_at(1, g)], r1[rows, group_at(2, g)], None
            )
            probs1[w * GROUPS + g] = p.astype(BF16)
            ctx1[rows, g * LANES : (g + 1) * LANES] = context.astype(BF16)
        pump(
            w,
            [functools.partial(gather_x, g) for g in (2, 3, 4)]
            + [functools.partial(gather_y, g) for g in (2, 3, 4)],
        )

    if plan.direct:
        mail.wait("gc2", "gd2", "gc3", "gd3")

    @pl.loop(0, TILES)
    def _(t):
        rows = tile_at(t)
        mixed = h0[rows, :].astype(F32) + dot(ctx1[rows, :], plan.load(wts, "O1"))
        h1[rows, :] = mixed
        scaled, _ = standardize(mixed)
        normed = (scaled * gains[1:2, :]).astype(BF16)
        m_s[rows, :] = normed
        upper = dot_nt(normed, plan.load(wts, "U"))
        coef = 0.7978845608028654
        square = upper * upper
        bent = jnp.tanh(coef * (upper + 0.044715 * (square * upper)))
        half_up = 0.5 * (1.0 + bent)
        active = (upper * half_up).astype(BF16)
        y_s[rows, :] = active
        slope[rows, :] = (
            half_up
            + 0.5 * upper * (1.0 - bent * bent) * (coef * (1.0 + 3 * 0.044715 * square))
        ).astype(BF16)
        allh[aligned(half * 864 + t * TILE, TILE), :] = (
            mixed + dot(active, plan.load(wts, "V"))
        ).astype(BF16)

    mail.start("h2")
    allh[13 * WSZ :, :] = jnp.zeros((allh.shape[0] - 13 * WSZ, D), BF16)
    small_own = small.at[0] if plan.direct else r.tail
    small_own[...] = jnp.zeros((8, D), F32)
    if plan.direct:
        mail.wait("gc4", "gd4")
    mail.wait("h2")

    h2, c_s, r2, ctx2, dctx = r.h2, r.c, r.r2, r.ctx2, r.dctx
    probs2, dh3_s, f_s, dpred_s, dr2 = r.probs2, r.dh3, r.f, r.dpred, r2
    scale = r.scale[0:1, :]

    @pl.loop(0, TILES)
    def _(t):
        rows = tile_at(t)
        spots = column[rows, :]
        for b in range(1920 // LANES):
            picks[:, b * LANES : (b + 1) * LANES] = jnp.where(
                spots == order_row[:, b * LANES : (b + 1) * LANES], 1.0, 0.0
            ).astype(BF16)
        hidden = dot(picks[:, :1920], allh[...])
        h2[rows, :] = hidden.astype(BF16)
        scaled, _ = standardize(hidden)
        normed = (scaled * gains[2:3, :]).astype(BF16)
        c_s[rows, :] = normed
        r2[rows, :] = dot_nt(normed, plan.load(wts, "A2")).astype(BF16)

    def same_column():
        key = lax.broadcasted_iota(jnp.int32, (PACK, CROWS, CROWS), 1)
        ask = lax.broadcasted_iota(jnp.int32, (PACK, CROWS, CROWS), 2)
        keep = (lax.bitwise_and(key, 7) == lax.bitwise_and(ask, 7)) & (key < LEV * 8)
        return keep.reshape(PACK * CROWS, CROWS)

    @pl.loop(0, CHUNKS)
    def _(k):
        rows = pl.ds(pl.multiple_of(k * CROWS, 16), CROWS)
        keep = same_column()
        for g in range(GROUPS):
            p, context = attend(
                r2[rows, group_at(0, g)], r2[rows, group_at(1, g)], r2[rows, group_at(2, g)], keep
            )
            probs2[k * GROUPS + g] = p.astype(probs2.dtype)
            ctx2[rows, g * LANES : (g + 1) * LANES] = context.astype(BF16)

    @pl.loop(0, TILES)
    def _(t):
        rows = tile_at(t)
        o2 = plan.load(wts, "O2")
        deq = plan.load(wts, "Q")
        hidden = (h2[rows, :].astype(F32) + dot(ctx2[rows, :], o2)).astype(BF16).astype(F32)
        scaled, spread = standardize(hidden)
        normed = (scaled * gains[3:4, :]).astype(BF16)
        f_s[rows, :] = normed
        error = dot_nt(normed, deq) - velocity[rows, :]
        weighed = token_w[rows, :] * error
        small_own[5:6, 0:PIN] += jnp.sum(weighed * error, axis=0, keepdims=True) * scale
        dpred = (2.0 * scale * weighed).astype(BF16)
        dpred_s[rows, :] = dpred
        upstream = dot(dpred, deq)
        small_own[3:4, :] += jnp.sum(upstream * scaled, axis=0, keepdims=True)
        dh3 = standardize_back(scaled, spread, gains[3:4, :], upstream).astype(BF16)
        dh3_s[rows, :] = dh3
        dctx[rows, :] = dot_nt(dh3, o2).astype(BF16)

    plan.store(grads, "Q", dot_tn(dpred_s[...], f_s[...]))
    plan.store(grads, "O2", dot_tn(ctx2[...], dh3_s[...]))

    @pl.loop(0, CHUNKS)
    def _(k):
        rows = pl.ds(pl.multiple_of(k * CROWS, 16), CROWS)
        for g in range(GROUPS):
            parts = attend_back(
                probs2[k * GROUPS + g],
                r2[rows, group_at(0, g)],
                r2[rows, group_at(1, g)],
                r2[rows, group_at(2, g)],
                dctx[rows, g * LANES : (g + 1) * LANES],
            )
            for i, part in enumerate(parts):
                dr2[rows, group_at(i, g)] = part.astype(BF16)

    @pl.loop(0, TILES)
    def _(t):
        rows = tile_at(t)
        upstream = dot(dr2[rows, :], plan.load(wts, "A2"))
        scaled, spread = standardize(h2[rows, :].astype(F32))
        small_own[2:3, :] += jnp.sum(upstream * scaled, axis=0, keepdims=True)
        back = standardize_back(scaled, spread, gains[2:3, :], upstream)
        everyone[aligned(base + t * TILE, TILE), :] = (
            dh3_s[rows, :].astype(F32) + back
        ).astype(BF16)

    mail.start("dh2")
    everyone[2 * ROWS :, :] = jnp.zeros((everyone.shape[0] - 2 * ROWS, D), BF16)
    plan.store(grads, "A2", dot_tn(dr2[...], c_s[...]))
    direct(mail.start, "Lc")
    mail.wait("dh2")

    dh2_s, do_s, dh0_s, dr1, du_s, dh1_s = c_s, f_s, dh3_s, r1, slope, r.dh1

    @pl.loop(0, TILES)
    def _(t):
        rows = tile_at(t)
        spots = order_col[aligned(half * 864 + t * TILE, TILE), :]
        row = lax.broadcasted_iota(jnp.int32, (TILE, LANES), 0) + t * TILE
        spots = jnp.where(row < WSZ * half, -1, spots)
        for b in range(2048 // LANES):
            picks[:, b * LANES : (b + 1) * LANES] = jnp.where(
                spots == r.both[:, b * LANES : (b + 1) * LANES], 1.0, 0.0
            ).astype(BF16)
        dh2 = dot(picks[...], everyone[...])
        low = dh2.astype(BF16)
        dh2_s[rows, :] = low
        du = (dot_nt(low, plan.load(wts, "V")) * slope[rows, :].astype(F32)).astype(BF16)
        du_s[rows, :] = du
        upstream = dot(du, plan.load(wts, "U"))
        scaled, spread = standardize(h1[rows, :])
        small_own[1:2, :] += jnp.sum(upstream * scaled, axis=0, keepdims=True)
        dh1 = dh2 + standardize_back(scaled, spread, gains[1:2, :], upstream)
        dh1_s[rows, :] = dh1
        do = dh1.astype(BF16)
        do_s[rows, :] = do
        dctx[rows, :] = dot_nt(do, plan.load(wts, "O1")).astype(BF16)
        pump(t, [functools.partial(sum_pair, "L"), None, functools.partial(sum_plane, "L")])

    for i in range(4):
        part = slice(i * D, (i + 1) * D)
        plan.store_part(grads, "V", i, dot_tn(y_s[:, part], dh2_s[...]))
    direct(mail.start, "Vc")
    for i in range(4):
        part = slice(i * D, (i + 1) * D)
        plan.store_part(grads, "U", i, dot_tn(du_s[:, part], m_s[...]))
    direct(mail.start, "Uc")
    plan.store(grads, "O1", dot_tn(ctx1[...], do_s[...]))
    direct(sum_pair, "V")
    direct(sum_ring, "L")

    @pl.loop(0, WINS)
    def _(w):
        rows = pl.ds(pl.multiple_of(w * WSZ, 16), WSZ)
        for g in range(GROUPS):
            parts = attend_back(
                probs1[w * GROUPS + g],
                r1[rows, group_at(0, g)],
                r1[rows, group_at(1, g)],
                r1[rows, group_at(2, g)],
                dctx[rows, g * LANES : (g + 1) * LANES],
            )
            for i, part in enumerate(parts):
                dr1[rows, group_at(i, g)] = part.astype(BF16)
        pump(
            w,
            [
                functools.partial(sum_pair, "U"),
                None,
                functools.partial(sum_plane, "V"),
                None,
                functools.partial(sum_ring, "V"),
                functools.partial(sum_plane, "U"),
                None,
            ],
        )

    plan.store(grads, "A1", dot_tn(dr1[...], a_s[...]))
    direct(mail.start, "Nc")

    @pl.loop(0, TILES)
    def _(t):
        rows = tile_at(t)
        upstream = dot(dr1[rows, :], plan.load(wts, "A1"))
        scaled, spread = standardize(h0[rows, :].astype(F32))
        small_own[0:1, :] += jnp.sum(upstream * scaled, axis=0, keepdims=True)
        back = standardize_back(scaled, spread, gains[0:1, :], upstream)
        dh0 = (dh1_s[rows, :] + back).astype(BF16)
        dh0_s[rows, :] = dh0
        small_own[4:5, :] += ftime * jnp.sum(dh0.astype(F32), axis=0, keepdims=True)
        pump(t, [functools.partial(sum_ring, "U"), functools.partial(sum_pair, "N"), None])

    plan.store(grads, "E", dot_tn(joined[...], dh0_s[...]))
    if not plan.direct:
        out = pltpu.make_async_copy(grads.at[0, 0], r.grads_out, local_sems.at[15])
        out.start()
        out.wait()
        mail.close()
        return

    grads[:, :, 48:64, :] = jnp.zeros((4, 2, 16, D), BF16)
    mail.start("Oc", "sc")
    sum_plane("N")
    mail.wait("sc")
    small[1] = small[0] + small_c[...]
    mail.start("sp0", "sp1", "sp2")
    sum_pair("O")
    sum_ring("N")
    mail.wait("sp0", "sp1", "sp2")
    small_z[z] = (small[1] + small_p[0]) + (small_p[1] + small_p[2])
    mail.start("sz0", "sz1", "sz2")
    sum_plane("O")
    mail.wait("sz0", "sz1", "sz2")
    r.tail[...] = ((small_z[0] + small_z[1]) + small_z[2]) + small_z[3]
    sum_ring("O")
    for key in SUMS:
        mail.wait(*(f"{key}g{k}" for k in range(3)))
    squares = jnp.zeros((16, D), F32)
    at_row = 0
    for name, width in zip(NAMES, WIDTHS):
        size = width // SHARDS
        part = final[PACKED[name] : PACKED[name] + size, :]
        r.total[at_row : at_row + size, :] = part
        part = part.astype(F32)
        squares = squares + jnp.sum((part * part).reshape(size // 16, 16, D), axis=0)
        at_row += size
    norm = jnp.sum(jnp.sum(squares, axis=1, keepdims=True), axis=0, keepdims=True)
    square[dp] = jnp.broadcast_to(norm, (8, LANES))
    mail.start(*(f"n{k}" for k in range(1, SHARDS)))
    mail.wait(*(f"n{k}" for k in range(1, SHARDS)))
    norm = square[0]
    for k in range(1, SHARDS):
        norm = norm + square[k]
    r.norm[...] = norm
    mail.close()


def adam_update(param, grad, first, second, average, correction, decay_rate, rate):
    first_new = BETA * first + (1.0 - BETA) * grad
    second_new = BETA * second + (1.0 - BETA) * grad * grad
    direction = first_new / correction / (jnp.sqrt(second_new / correction) + EPS_ADAM)
    param_new = param - rate * (direction + decay_rate * param)
    average_new = EMA_RATE * average + (1.0 - EMA_RATE) * param_new
    return (param_new, first_new, second_new, average_new)


def update_kernel(
    step, tail, norm, total, master, first, second, average, gains, gain_first, gain_second, gain_average,
    loss_out, norm_out, new_w, new_f, new_s, new_a, low, new_g, new_gf, new_gs, new_ga,
):
    gain_grad = tail[0:5, :]
    square = jnp.sum(jnp.sum(gain_grad * gain_grad, axis=1, keepdims=True), axis=0, keepdims=True)
    size = jnp.sqrt(norm[0:1, 0:1] + square)
    factor = jnp.minimum(1.0, CLIP_MAX / (size + 1e-06))
    steps = jnp.full((1, 1), step[0].astype(F32), F32)
    correction = 1.0 - jnp.exp2(-steps)
    results = adam_update(
        master[...], factor * total[...].astype(F32), first[...], second[...], average[...],
        correction, DECAY_WEIGHT, RATE,
    )
    for ref, value in zip((new_w, new_f, new_s, new_a), results):
        ref[...] = value
    low[...] = results[0].astype(BF16)

    @pl.when(pl.program_id(0) == 0)
    def _():
        norm_out[...] = size
        loss_out[...] = jnp.sum(tail[5:6, 0:PIN], axis=1, keepdims=True)
        results = adam_update(
            gains[...], factor * gain_grad, gain_first[...], gain_second[...], gain_average[...],
            correction, 0.0, GAIN_RATE,
        )
        for ref, value in zip((new_g, new_gf, new_gs, new_ga), results):
            ref[...] = value


def column_table():
    row = np.arange(1024)
    chunk, inner = row // CROWS, row % CROWS
    level, col = inner // 8, inner % 8
    token = level * WSZ + chunk * 16 + col
    return np.where((row < ROWS) & (level < LEV), token, -9).astype(np.int32)


def shape_of(rows, columns, dtype):
    return jax.ShapeDtypeStruct((rows, columns), dtype)


def local(
    noise_draw, single_step, double_step, state_now, target_flag, flow_time, live_count,
    latitude_row, window_order, latitude_weight, level_weight, step_count,
    master_weights, first_moment, second_moment, average_weights,
    gain_rows, gain_first, gain_second, gain_average,
):
    micro = noise_draw.shape[0]
    tokens = noise_draw.shape[1]
    members = lax.axis_size("dp")
    plan = Plan(members == SHARDS)
    smem = pl.BlockSpec(memory_space=pltpu.SMEM)
    vmem = pl.BlockSpec(memory_space=pltpu.VMEM)
    anym = pl.BlockSpec(memory_space=pl.ANY)
    table = column_table()
    both = np.full((2048,), -8, np.int32)
    for h in range(2):
        both[h * ROWS : (h + 1) * ROWS] = np.where(table[:ROWS] >= 0, table[:ROWS] + 8 * h, -8)

    inputs = dict(
        noise=(noise_draw, anym),
        single=(single_step, anym),
        double=(double_step, anym),
        state=(state_now, anym),
        flag=(target_flag.T, smem),
        ftime=(flow_time.T, smem),
        live=(live_count.T, smem),
        lat_row=(latitude_row, vmem),
        order=(window_order, vmem),
        lat_weight=(latitude_weight, smem),
        lev_weight=(level_weight, smem),
        gains=(gain_rows, vmem),
        table=(jnp.asarray(table)[None, :], vmem),
        both=(jnp.asarray(both)[None, :], vmem),
    )
    if plan.direct:
        inputs |= dict(master=(master_weights, anym))
        outputs = dict(
            total=(shape_of(master_weights.shape[0], D, BF16), vmem),
            tail=(shape_of(8, D, F32), vmem),
            norm=(shape_of(8, LANES, F32), vmem),
        )
    else:
        gathered = lax.all_gather(master_weights.astype(BF16), "dp", axis=0, tiled=True)
        inputs |= dict(weights_in=(natural_order(gathered, members), anym))
        lat_match = latitude_row[:, :, None] == jnp.arange(LATN, dtype=jnp.int32)[None, None, :]
        lat_values = jnp.sum(
            jnp.where(lat_match, latitude_weight.astype(F32)[None, None, :], 0.0), axis=2
        )
        weigh = (level_weight.astype(F32)[None, :, None] * lat_values[:, None, :]).reshape(
            micro, tokens
        ) * 1e-06
        alive = jnp.arange(tokens, dtype=jnp.int32)[None, :] < live_count
        total = lax.psum(jnp.sum(jnp.where(alive, weigh, 0.0)), "dp")
        inputs |= dict(scale_in=(jnp.full((8, LANES), 1.0 / (PIN * total), F32), vmem))
        outputs = dict(
            grads_out=(shape_of(plan.rows, D, BF16), anym),
            tail=(shape_of(8, D, F32), vmem),
        )
    scratch = dict(
        wts=pltpu.VMEM((*plan.shape, plan.rows, D), BF16),
        grads=pltpu.VMEM((*plan.shape, plan.rows, D), BF16),
        raw=pltpu.VMEM((tokens, PIN), BF16),
        source=pltpu.VMEM((1920, D), BF16),
        picks=pltpu.VMEM((TILE, 2048), BF16),
        order_row=pltpu.VMEM((1, 1920), jnp.int32),
        order_col=pltpu.VMEM((1920, LANES), jnp.int32),
        column=pltpu.VMEM((1024, LANES), jnp.int32),
        token_w=pltpu.VMEM((ROWS, LANES), F32),
        lat_col=pltpu.VMEM((256, LANES), F32),
        scale=pltpu.VMEM((8, LANES), F32),
        velocity=pltpu.VMEM((ROWS, PIN), F32),
        joined=pltpu.VMEM((ROWS, 2 * PIN), BF16),
        h0=pltpu.VMEM((ROWS, D), BF16),
        a=pltpu.VMEM((ROWS, D), BF16),
        r1=pltpu.VMEM((ROWS, 3 * D), BF16),
        probs1=pltpu.VMEM((WINS * GROUPS, PACK * WSZ, WSZ), BF16),
        ctx1=pltpu.VMEM((ROWS, D), BF16),
        h1=pltpu.VMEM((ROWS, D), F32),
        m=pltpu.VMEM((ROWS, D), BF16),
        slope=pltpu.VMEM((ROWS, FF), BF16),
        y=pltpu.VMEM((ROWS, FF), BF16),
        allh=pltpu.VMEM((1920, D), BF16),
        h2=pltpu.VMEM((ROWS, D), BF16),
        c=pltpu.VMEM((ROWS, D), BF16),
        r2=pltpu.VMEM((ROWS, 3 * D), BF16),
        probs2=pltpu.VMEM((CHUNKS * GROUPS, PACK * CROWS, CROWS), BF16),
        ctx2=pltpu.VMEM((ROWS, D), BF16),
        dctx=pltpu.VMEM((ROWS, D), BF16),
        dh3=pltpu.VMEM((ROWS, D), BF16),
        f=pltpu.VMEM((ROWS, D), BF16),
        dpred=pltpu.VMEM((ROWS, PIN), BF16),
        everyone=pltpu.VMEM((2048, D), BF16),
        dh1=pltpu.VMEM((ROWS, D), F32),
        local_sems=pltpu.SemaphoreType.DMA((16,)),
        send_sems=pltpu.SemaphoreType.DMA((MESSAGES if plan.direct else 2,)),
        recv_sems=pltpu.SemaphoreType.DMA((MESSAGES if plan.direct else 2,)),
    )
    if plan.direct:
        scratch |= dict(
            tot=pltpu.VMEM((8, LANES), F32),
            tot_z=pltpu.VMEM((4, 8, LANES), F32),
            tot_x=pltpu.VMEM((8, LANES), F32),
            pair_in=pltpu.VMEM((4, 2, PACKED_ROWS // 2, D), BF16),
            plane_in=pltpu.VMEM((3, 4, PACKED_ROWS // 4, D), BF16),
            ring_out=pltpu.VMEM((4, PACKED_ROWS // 4, D), BF16),
            ring_in=pltpu.VMEM((4, PACKED_ROWS // 4, D), BF16),
            final=pltpu.VMEM((PACKED_ROWS, D), BF16),
            small=pltpu.VMEM((2, 8, D), F32),
            small_c=pltpu.VMEM((8, D), F32),
            small_p=pltpu.VMEM((3, 8, D), F32),
            small_z=pltpu.VMEM((4, 8, D), F32),
            square=pltpu.VMEM((SHARDS, 8, LANES), F32),
        )
    names = [*inputs, *outputs, *scratch]
    results = pl.pallas_call(
        functools.partial(step_kernel, plan, names),
        out_shape=[value[0] for value in outputs.values()],
        in_specs=[value[1] for value in inputs.values()],
        out_specs=[value[1] for value in outputs.values()],
        scratch_shapes=list(scratch.values()),
        compiler_params=pltpu.CompilerParams(
            vmem_limit_bytes=VMEM_MAX, collective_id=0, has_side_effects=True
        ),
        name="train_step",
    )(*(value[0] for value in inputs.values()))
    results = SimpleNamespace(**dict(zip(outputs, results)))
    if plan.direct:
        total, tail, norm = results.total, results.tail, results.norm
    else:
        grads = stored_order(results.grads_out.astype(F32), members)
        total = lax.psum_scatter(grads, "dp", scatter_dimension=0, tiled=True)
        total, tail = lax.psum(total, "pipe"), lax.psum(results.tail, ("dp", "pipe"))
        norm = jnp.full((8, LANES), lax.psum(jnp.sum(total * total), "dp"), F32)
    shard = master_weights.shape[0]
    steps = 3 if shard % 24 == 0 else 1
    block = shard // steps
    big = pl.BlockSpec((block, D), lambda i: (i, 0))
    one = pl.BlockSpec((1, 1), lambda i: (0, 0))
    row8 = pl.BlockSpec((8, D), lambda i: (0, 0))
    row5 = pl.BlockSpec((5, D), lambda i: (0, 0))
    outs = pl.pallas_call(
        update_kernel,
        grid=(steps,),
        out_shape=[shape_of(1, 1, F32)] * 2
        + [shape_of(shard, D, F32)] * 4
        + [shape_of(shard, D, BF16)]
        + [shape_of(5, D, F32)] * 4,
        in_specs=[smem, row8, pl.BlockSpec((8, LANES), lambda i: (0, 0))] + [big] * 5 + [row5] * 4,
        out_specs=[one] * 2 + [big] * 5 + [row5] * 4,
        compiler_params=pltpu.CompilerParams(vmem_limit_bytes=VMEM_MAX),
        name="update",
    )(
        step_count, tail, norm, total, master_weights, first_moment, second_moment, average_weights,
        gain_rows, gain_first, gain_second, gain_average,
    )
    return (outs[0][0, 0], outs[1][0, 0], *outs[2:])


def solution(mesh):
    over = P("dp", None)
    token = P(None, "dp", None)
    pair = P(None, "dp")
    in_specs = (token,) * 4 + (pair,) * 5 + (P(),) * 3 + (over,) * 4 + (P(),) * 4
    out_specs = (P(), P()) + (over,) * 5 + (P(),) * 4
    return jax.shard_map(local, mesh=mesh, in_specs=in_specs, out_specs=out_specs, check_vma=False)
```

time: 488 us -> 172 us (0.35)
  waiting for transfers between devices: 224 us -> 0 us
  blocking collectives: 85.9 us -> 0 us
  Pallas kernels: 110 us -> 170 us
  local copies, waits for them, and re-layouts: 29.5 us -> 0 us
  other arithmetic: 19.9 us -> 0 us
  between operations: 18.1 us -> 1.46 us
    reduce_scatter x1 -> x0, waiting for transfers between devices: 170 us -> none  [local(): lax.psum_scatter(grads, 'dp', scatter_dimension=0, tiled=True)]
    psum x3 -> x0, blocking collectives: 85.9 us -> none  [the longest x1 40 us: local(): lax.psum((gains_part, jnp.sum(small_late[2])), ('dp', 'pipe'))]
    pallas_call x3 -> x2, Pallas kernels: 110 us -> 170 us  [the longest x1 163 us: local(): pl.pallas_call(functools.partial(step_kernel, plan, names), out_shape=[va...]
    all_gather x1 -> x0, waiting for transfers between devices: 53.6 us -> none  [local(): lax.all_gather(master_weights.astype(BF16), 'dp', axis=0, tiled=True)]
    slice x15 -> x0, local copies, waits for them, and re-layouts: 15.3 us -> none  [the longest x7 6.72 us: stored_order(): natural[STARTS[number]:STARTS[number + 1]]]
    unnamed x47 -> x0, local copies, waits for them, and re-layouts: 10.1 us -> none
    convert_element_type x5 -> x0, other arithmetic: 7 us -> none  [the longest x1 4.21 us: local(): new_weights.astype(BF16)]
    reduce_sum x5 -> x0, other arithmetic: 5.06 us -> none  [the longest x1 2.32 us: local(): square_total = lax.psum(jnp.sum(shard * shard), 'dp')]
  transfers between devices with their start and end apart: 3 -> 0, of which waited for: 2 -> 0; matrix products, arithmetic and copies ran while one was open for 3% -> 0% of each run, Pallas kernels for 0% -> 0%
where the time goes in v2:
time: 172 us
  Pallas kernels  170 us (99%)
    pallas_call x1, Pallas kernels, local(): pl.pallas_call(functools.partial(step_kernel, plan, names), out_shape=[va...  163 us
    pallas_call x1, Pallas kernels, local(): pl.pallas_call(update_kernel, grid=(steps,), out_shape=[shape_of(1, 1, F3...  7.29 us

profile of v2, /device:TPU:0, one launch (start us, length us, event | category | flops | bytes accessed | tf_op | source)
XLA Modules:
  0.0 171.9 jit_solution(5130589540768620334)
XLA Ops:
  1.3 163.1 %train_step.1 = (bf16[816,384]{1,0:T(8,128)(2,1)}, f32[8,384]{1,0:T(8,128)}, f32[8,128]{1,0:T(8,128)}) custom-call(bf16[2,1872,128]{2,1,0:T(8,128)(2,1)} %refs_0_.1, bf16[2,1872,128]{2,1,0:T(8,128)(2,1)} %refs_1_.1, bf16[2,1872,128]{2,1,0:T(8,128)(2,1)} %refs_2_.1, bf16[2,1872,128]{2,1,0:T(8,128)(2,1)} %refs_3_.1, s32[1,2]{1,0:T(1,128)} %bitcast.5, ...), custom_call_target="tpu_custom_call" | custom-call | tf_op jit(solution)/shard_map/train_step/pallas_call | solution.py:982
  164.4 7.3 %update.1 = (f32[1,1]{1,0:T(1,128)}, f32[1,1]{1,0:T(1,128)}, f32[816,384]{1,0:T(8,128)}, f32[816,384]{1,0:T(8,128)}, f32[816,384]{1,0:T(8,128)}, /*index=5*/f32[...) custom-call(s32[1]{0:T(128)S(6)} %copy.33.step, ...), custom_call_target="tpu_custom_call" | custom-call | tf_op jit(solution)/shard_map/update/pallas_call | solution.py:1008

commit v3 on v2

--- a/solution.py
+++ b/solution.py
@@ -165,11 +165,23 @@
 
 WIDTHS = (2 * PIN, 3 * D, D, FF, FF, 3 * D, D, PIN)
 NAMES = ("E", "A1", "O1", "U", "V", "A2", "O2", "Q")
-PACKED = dict(E=0, Q=32, A1=64, O1=208, U=256, V=448, A2=640, O2=784)
+PACKED = dict(E=0, A1=48, O1=192, Q=240, U=256, V=448, A2=640, O2=784)
+SPARE = slice(32, 48)
 PACKED_ROWS = 832
 SHARDS = 8
-GATHERS = ((0, 64, False), (64, 192, False), (256, 192, True), (448, 192, True), (640, 192, True))
-SUMS = dict(L=(640, 192), V=(448, 192), U=(256, 192), N=(64, 192), O=(0, 64))
+GATHERS = (
+    (0, 64, False),
+    (64, 64, False),
+    (128, 64, False),
+    (192, 64, False),
+    (256, 192, True),
+    (448, 96, False),
+    (544, 96, False),
+    (640, 192, True),
+)
+SUMS = dict(
+    L=(640, 192), V=(448, 192), U=(256, 192), M=(192, 64), N=(64, 64), R=(128, 64), O=(0, 64)
+)
 
 
 class Plan:
@@ -235,7 +247,7 @@
             build().wait_send()
 
 
-MESSAGES = 120
+MESSAGES = 150
 
 
 def aligned(start, size):
@@ -417,6 +429,44 @@
         final[aligned(start + c * h + y * q, q), :] = total.astype(BF16)
         mail.start(*(f"{key}g{k}" for k in range(3)))
 
+    def gather_z(g):
+        mail.start(*(f"gz{g}{k}" for k in range(3)))
+
+    def gather_x(g):
+        mail.wait(*(f"gz{g}{k}" for k in range(3)))
+        if GATHERS[g][2]:
+            mail.start(f"gx{g}")
+        else:
+            mail.start(f"gx{g}", f"gc{g}")
+
+    def gather_y(g):
+        mail.wait(f"gx{g}")
+        if GATHERS[g][2]:
+            mail.start(f"gy{g}", f"gc{g}")
+        else:
+            mail.start(f"gd{g}")
+
+    def gather_core(g):
+        mail.wait(f"gy{g}")
+        mail.start(f"gd{g}")
+
+    def gathered(*groups):
+        for g in groups:
+            mail.wait(f"gc{g}", f"gd{g}")
+
+    def steps(*pairs):
+        def run():
+            for function, value in pairs:
+                function(value)
+
+        return run
+
+    def pump(index, *stages):
+        if plan.direct:
+            for k, stage in enumerate(stages):
+                if stage is not None:
+                    pl.when(index == k)(stage)
+
     def direct(function, *values):
         if plan.direct:
             function(*values)
@@ -441,10 +491,11 @@
         mail.start("tz0", "tz1", "tz2")
         for name in NAMES:
             loads["w" + name].wait()
-        r.h1[48:64, :] = jnp.zeros((16, D), F32)
+        r.h1[SPARE, :] = jnp.zeros((16, D), F32)
         for g, mine in enumerate(own):
             wts[z, x, mine, :] = r.h1[mine, :].astype(BF16)
-            mail.start(*(f"gz{g}{k}" for k in range(3)))
+            if g < 2:
+                gather_z(g)
 
     order_row, order_col = r.order_row, r.order_col
     order_row[...] = jnp.full(order_row.shape, -1, jnp.int32)
@@ -470,6 +521,7 @@
     source[tokens:, :] = jnp.zeros((source.shape[0] - tokens, D), BF16)
     source[:tokens, PIN : 2 * PIN] = source[:tokens, PIN : 2 * PIN] * first + raw[...] * second
     lane = lax.broadcasted_iota(jnp.int32, (1, LANES), 1)
+    direct(steps((gather_x, 0), (gather_z, 2)))
 
     @pl.loop(0, TILES)
     def _(t):
@@ -483,14 +535,17 @@
         noisy = (1.0 - ftime) * drawn[:, 0:PIN] + ftime * drawn[:, PIN : 2 * PIN]
         joined[rows, 0:PIN] = noisy.astype(BF16)
         joined[rows, PIN:] = drawn[:, 2 * PIN :].astype(BF16)
+        pump(
+            t,
+            steps((gather_x, 1), (gather_z, 3)),
+            steps((gather_x, 2), (gather_z, 4)),
+            steps((gather_y, 0)),
+        )
 
     if plan.direct:
         mail.wait("tz0", "tz1", "tz2")
         tot[...] = ((tot_z[0] + tot_z[1]) + tot_z[2]) + tot_z[3]
         mail.start("tx")
-        for g in (0, 1):
-            mail.wait(*(f"gz{g}{k}" for k in range(3)))
-            mail.start(f"gx{g}", f"gc{g}")
 
     @pl.loop(0, CHUNKS)
     def _(k):
@@ -510,15 +565,13 @@
         token_w[rows, :] = jnp.zeros((8, LANES), F32)
 
     if plan.direct:
-        for g in (2, 3, 4):
-            mail.wait(*(f"gz{g}{k}" for k in range(3)))
-            mail.start(f"gx{g}")
+        gather_y(1)
+        gather_x(3)
+        gather_z(5)
         mail.wait("tx")
         r.scale[...] = 1.0 / (PIN * (tot[...] + r.tot_x[...]))
-        for g in (0, 1):
-            mail.wait(f"gx{g}")
-            mail.start(f"gd{g}")
-        mail.wait("gc0", "gd0", "gc1", "gd1")
+        gather_y(2)
+        gathered(0, 1, 2)
     else:
         r.scale[...] = jnp.broadcast_to(r.scale_in[0:1, :], (8, LANES))
         loads["w"].wait()
@@ -535,20 +588,12 @@
         normed = (scaled * gains[0:1, :]).astype(BF16)
         a_s[rows, :] = normed
         r1[rows, :] = dot_nt(normed, plan.load(wts, "A1")).astype(BF16)
-
-    def gather_x(g):
-        mail.wait(f"gx{g}")
-        mail.start(f"gy{g}", f"gc{g}")
-
-    def gather_y(g):
-        mail.wait(f"gy{g}")
-        mail.start(f"gd{g}")
-
-    def pump(index, steps):
-        if plan.direct:
-            for k, step in enumerate(steps):
-                if step is not None:
-                    pl.when(index == k)(step)
+        pump(
+            t,
+            steps((gather_y, 3)),
+            steps((gather_x, 4), (gather_z, 6)),
+            steps((gather_x, 5), (gather_z, 7)),
+        )
 
     @pl.loop(0, WINS)
     def _(w):
@@ -561,12 +606,16 @@
             ctx1[rows, g * LANES : (g + 1) * LANES] = context.astype(BF16)
         pump(
             w,
-            [functools.partial(gather_x, g) for g in (2, 3, 4)]
-            + [functools.partial(gather_y, g) for g in (2, 3, 4)],
-        )
-
-    if plan.direct:
-        mail.wait("gc2", "gd2", "gc3", "gd3")
+            steps((gather_y, 4)),
+            steps((gather_x, 6)),
+            steps((gather_y, 5)),
+            steps((gather_x, 7)),
+            steps((gather_y, 6)),
+            steps((gather_core, 4)),
+            steps((gather_y, 7)),
+        )
+
+    direct(gathered, 3, 4, 5, 6)
 
     @pl.loop(0, TILES)
     def _(t):
@@ -596,7 +645,8 @@
     small_own = small.at[0] if plan.direct else r.tail
     small_own[...] = jnp.zeros((8, D), F32)
     if plan.direct:
-        mail.wait("gc4", "gd4")
+        gather_core(7)
+        gathered(7)
     mail.wait("h2")
 
     h2, c_s, r2, ctx2, dctx = r.h2, r.c, r.r2, r.ctx2, r.dctx
@@ -701,32 +751,37 @@
             picks[:, b * LANES : (b + 1) * LANES] = jnp.where(
                 spots == r.both[:, b * LANES : (b + 1) * LANES], 1.0, 0.0
             ).astype(BF16)
-        dh2 = dot(picks[...], everyone[...])
-        low = dh2.astype(BF16)
-        dh2_s[rows, :] = low
+        dh2_s[rows, :] = dot(picks[...], everyone[...]).astype(BF16)
+
+    for i in range(4):
+        part = slice(i * D, (i + 1) * D)
+        plan.store_part(grads, "V", i, dot_tn(y_s[:, part], dh2_s[...]))
+    direct(mail.start, "Vc")
+    direct(sum_pair, "L")
+
+    @pl.loop(0, TILES)
+    def _(t):
+        rows = tile_at(t)
+        low = dh2_s[rows, :]
         du = (dot_nt(low, plan.load(wts, "V")) * slope[rows, :].astype(F32)).astype(BF16)
         du_s[rows, :] = du
         upstream = dot(du, plan.load(wts, "U"))
         scaled, spread = standardize(h1[rows, :])
         small_own[1:2, :] += jnp.sum(upstream * scaled, axis=0, keepdims=True)
-        dh1 = dh2 + standardize_back(scaled, spread, gains[1:2, :], upstream)
+        dh1 = low.astype(F32) + standardize_back(scaled, spread, gains[1:2, :], upstream)
         dh1_s[rows, :] = dh1
         do = dh1.astype(BF16)
         do_s[rows, :] = do
         dctx[rows, :] = dot_nt(do, plan.load(wts, "O1")).astype(BF16)
-        pump(t, [functools.partial(sum_pair, "L"), None, functools.partial(sum_plane, "L")])
-
-    for i in range(4):
-        part = slice(i * D, (i + 1) * D)
-        plan.store_part(grads, "V", i, dot_tn(y_s[:, part], dh2_s[...]))
-    direct(mail.start, "Vc")
+        pump(t, steps((sum_pair, "V")))
+
     for i in range(4):
         part = slice(i * D, (i + 1) * D)
         plan.store_part(grads, "U", i, dot_tn(du_s[:, part], m_s[...]))
     direct(mail.start, "Uc")
     plan.store(grads, "O1", dot_tn(ctx1[...], do_s[...]))
-    direct(sum_pair, "V")
-    direct(sum_ring, "L")
+    direct(mail.start, "Mc")
+    direct(sum_plane, "L")
 
     @pl.loop(0, WINS)
     def _(w):
@@ -743,19 +798,18 @@
                 dr1[rows, group_at(i, g)] = part.astype(BF16)
         pump(
             w,
-            [
-                functools.partial(sum_pair, "U"),
-                None,
-                functools.partial(sum_plane, "V"),
-                None,
-                functools.partial(sum_ring, "V"),
-                functools.partial(sum_plane, "U"),
-                None,
-            ],
+            steps((sum_pair, "U"), (sum_pair, "M")),
+            steps((sum_ring, "L")),
+            steps((sum_plane, "V")),
+            None,
+            steps((sum_ring, "V")),
+            steps((sum_plane, "U")),
+            steps((sum_plane, "M")),
         )
 
     plan.store(grads, "A1", dot_tn(dr1[...], a_s[...]))
-    direct(mail.start, "Nc")
+    direct(mail.start, "Nc", "Rc")
+    direct(sum_ring, "U")
 
     @pl.loop(0, TILES)
     def _(t):
@@ -767,7 +821,7 @@
         dh0 = (dh1_s[rows, :] + back).astype(BF16)
         dh0_s[rows, :] = dh0
         small_own[4:5, :] += ftime * jnp.sum(dh0.astype(F32), axis=0, keepdims=True)
-        pump(t, [functools.partial(sum_ring, "U"), functools.partial(sum_pair, "N"), None])
+        pump(t, steps((sum_pair, "N"), (sum_pair, "R")), steps((sum_ring, "M")))
 
     plan.store(grads, "E", dot_tn(joined[...], dh0_s[...]))
     if not plan.direct:
@@ -777,32 +831,40 @@
         mail.close()
         return
 
-    grads[:, :, 48:64, :] = jnp.zeros((4, 2, 16, D), BF16)
+    grads[:, :, SPARE, :] = jnp.zeros((4, 2, 16, D), BF16)
     mail.start("Oc", "sc")
     sum_plane("N")
     mail.wait("sc")
     small[1] = small[0] + small_c[...]
     mail.start("sp0", "sp1", "sp2")
     sum_pair("O")
+    sum_plane("R")
     sum_ring("N")
+
+    def hand_out(squares, names):
+        for name in names:
+            number = NAMES.index(name)
+            spot, size = STARTS[number] // SHARDS, WIDTHS[number] // SHARDS
+            part = final[PACKED[name] : PACKED[name] + size, :]
+            r.total[spot : spot + size, :] = part
+            part = part.astype(F32)
+            squares = squares + jnp.sum((part * part).reshape(size // 16, 16, D), axis=0)
+        return squares
+
+    for key in ("L", "V", "U", "M"):
+        mail.wait(*(f"{key}g{k}" for k in range(3)))
+    squares = hand_out(jnp.zeros((16, D), F32), NAMES[2:])
     mail.wait("sp0", "sp1", "sp2")
     small_z[z] = (small[1] + small_p[0]) + (small_p[1] + small_p[2])
     mail.start("sz0", "sz1", "sz2")
     sum_plane("O")
+    sum_ring("R")
     mail.wait("sz0", "sz1", "sz2")
     r.tail[...] = ((small_z[0] + small_z[1]) + small_z[2]) + small_z[3]
     sum_ring("O")
-    for key in SUMS:
+    for key in ("N", "R", "O"):
         mail.wait(*(f"{key}g{k}" for k in range(3)))
-    squares = jnp.zeros((16, D), F32)
-    at_row = 0
-    for name, width in zip(NAMES, WIDTHS):
-        size = width // SHARDS
-        part = final[PACKED[name] : PACKED[name] + size, :]
-        r.total[at_row : at_row + size, :] = part
-        part = part.astype(F32)
-        squares = squares + jnp.sum((part * part).reshape(size // 16, 16, D), axis=0)
-        at_row += size
+    squares = hand_out(squares, NAMES[:2])
     norm = jnp.sum(jnp.sum(squares, axis=1, keepdims=True), axis=0, keepdims=True)
     square[dp] = jnp.broadcast_to(norm, (8, LANES))
     mail.start(*(f"n{k}" for k in range(1, SHARDS)))

time: 172 us -> 146 us (0.85)
  Pallas kernels: 170 us -> 144 us
    pallas_call x1, Pallas kernels: 163 us -> 137 us  [local(): pl.pallas_call(functools.partial(step_kernel, plan, names), out_shape=[va...]
where the time goes in v3:
time: 146 us
  Pallas kernels  144 us (99%)
  between operations  1.46 us (1%)
    pallas_call x1, Pallas kernels, local(): pl.pallas_call(functools.partial(step_kernel, plan, names), out_shape=[va...  137 us
    pallas_call x1, Pallas kernels, local(): pl.pallas_call(update_kernel, grid=(steps,), out_shape=[shape_of(1, 1, F3...  7.29 us

profile of v3, /device:TPU:0, one launch (start us, length us, event | category | flops | bytes accessed | tf_op | source)
XLA Modules:
  0.0 145.8 jit_solution(5365320088836538294)
XLA Ops:
  1.3 137.1 %train_step.1 = (bf16[816,384]{1,0:T(8,128)(2,1)}, f32[8,384]{1,0:T(8,128)}, f32[8,128]{1,0:T(8,128)}) custom-call(bf16[2,1872,128]{2,1,0:T(8,128)(2,1)} %refs_0_.1, bf16[2,1872,128]{2,1,0:T(8,128)(2,1)} %refs_1_.1, bf16[2,1872,128]{2,1,0:T(8,128)(2,1)} %refs_2_.1, bf16[2,1872,128]{2,1,0:T(8,128)(2,1)} %refs_3_.1, s32[1,2]{1,0:T(1,128)} %bitcast.5, ...), custom_call_target="tpu_custom_call" | custom-call | tf_op jit(solution)/shard_map/train_step/pallas_call | solution.py:1044
  138.4 7.3 %update.1 = (f32[1,1]{1,0:T(1,128)}, f32[1,1]{1,0:T(1,128)}, f32[816,384]{1,0:T(8,128)}, f32[816,384]{1,0:T(8,128)}, f32[816,384]{1,0:T(8,128)}, /*index=5*/f32[...) custom-call(s32[1]{0:T(128)S(6)} %copy.33.step, ...), custom_call_target="tpu_custom_call" | custom-call | tf_op jit(solution)/shard_map/update/pallas_call | solution.py:1070
